TPU v7x, 512 devices: a whole 4x8x8 slice. The times are simulated.
512 devices in a mesh: patch: 32 (over x, y), group: 16 (over z, core).
Axes of the slice: x: 4, y: 8, z: 8, core: 2. Of those that a mesh axis runs over, the one named last changes fastest.
Arguments:
- grid_latent: bfloat16 [262144, 512], P(('patch', 'group')), may hold values from -6 to 6
- mesh_latent: bfloat16 [131072, 512], P(('patch', 'group')), may hold values from -6 to 6
- cotangent: bfloat16 [131072, 512], P(('patch', 'group')), may hold values from -6 to 6
- halo_rows: int32 [131072], P(('patch', 'group')), may hold values from 0 to 511
- encoder_sender: int32 [393216], P(('patch', 'group')), may hold values from 0 to 767
- encoder_target: int32 [393216], P(('patch', 'group')), may hold values from 0 to 255
- encoder_count: int32 [512], P(('patch', 'group')), may hold values from 96 to 768, as said below
- process_sender: int32 [393216], P(('patch', 'group')), may hold values from 0 to 511
- process_target: int32 [393216], P(('patch', 'group')), may hold values from 0 to 255
- process_count: int32 [512], P(('patch', 'group')), may hold values from 96 to 768, as said below
- encoder_source: bfloat16 [512, 512], replicated, may hold values from -0.25 to 0.25
- encoder_dest: bfloat16 [512, 512], replicated, may hold values from -0.25 to 0.25
- encoder_output: bfloat16 [512, 512], replicated, may hold values from -0.25 to 0.25
- encoder_gain: float32 [512], replicated, may hold values from 0.5 to 1.5
- process_source: bfloat16 [512, 512], replicated, may hold values from -0.25 to 0.25
- process_dest: bfloat16 [512, 512], replicated, may hold values from -0.25 to 0.25
- process_output: bfloat16 [512, 512], replicated, may hold values from -0.25 to 0.25
- process_gain: float32 [512], replicated, may hold values from 0.5 to 1.5
Outputs:
- grid_grad: bfloat16 [262144, 512], P(('patch', 'group'))
- mesh_grad: bfloat16 [131072, 512], P(('patch', 'group'))
Inputs may be any that keep to these rules, and one draw needn't show every extreme that they name: `halo_rows`: a block's entries are rows of its own grid nodes. `encoder_sender`: rows of the block's extended grid table. `encoder_target`: rows of the block's own mesh nodes. The first encoder_count slots of a block are edges, the rest padding; some block is full in every draw. `process_sender`: rows of the block's sender table: its own mesh nodes, then the coarse nodes of its group. `process_target`: rows of the block's own mesh nodes. The first process_count slots of a block are edges, the rest padding; some block is full in every draw.
All inputs are finite; a program needn't handle non-finite values.
Results may differ from a plain program's by a relative error of at most 0.01.
Values may be sent and summed in bfloat16 or wider, within the bound.
A program may use at most 64 MiB of HBM per device.

v0:
```python
import jax
import jax.numpy as jnp
from jax import lax
from jax.sharding import PartitionSpec as P

EPSILON = 1e-05


def padded_2(x, sides, width):
    for axis, dim in sides:
        size, length = (lax.axis_size(axis), x.shape[dim])
        up = [(i, (i + 1) % size) for i in range(size)]
        down = [(j, i) for i, j in up]
        last = lax.slice_in_dim(x, length - width, length, axis=dim)
        initial = lax.slice_in_dim(x, 0, width, axis=dim)
        before = lax.ppermute(last, axis, up)
        after = lax.ppermute(initial, axis, down)
        x = jnp.concatenate([before, x, after], axis=dim)
    return x


def from_everyone(x, axis):
    copies = jnp.broadcast_to(x, (lax.axis_size(axis), *x.shape))
    return lax.all_to_all(copies, axis, split_axis=0, concat_axis=0, tiled=True)


def laid_out(parts, dim):
    parts = jnp.moveaxis(parts, 0, dim)
    shape = parts.shape
    return parts.reshape(*shape[:dim], shape[dim] * shape[dim + 1], *shape[dim + 2 :])


def gathered_copies(x, axis, dim):
    parts = from_everyone(x, axis)
    return laid_out(parts, dim)


def cut_along(x, dim, length):
    before, after = (x.shape[:dim], x.shape[dim + 1 :])
    return jnp.moveaxis(x.reshape(*before, length, -1, *after), dim, 0)


def sum_at_owner(x, axis, dim):
    length = lax.axis_size(axis)
    parts = lax.all_to_all(cut_along(x, dim, length), axis, 0, 0, tiled=True)
    return jnp.sum(parts, axis=0)


def silu_slope(values):
    logistic = jax.nn.sigmoid(values)
    return logistic * (1.0 + values * (1.0 - logistic))


def norm_forward(values, norm_gain):
    center = values - jnp.mean(values, axis=-1, keepdims=True)
    inverse = lax.rsqrt(jnp.mean(center * center, axis=-1, keepdims=True) + EPSILON)
    normed = center * inverse
    return (normed * norm_gain, normed, inverse)


def norm_backward(grad_out, normed, inverse, norm_gain):
    scaled = grad_out * norm_gain
    return inverse * (
        scaled
        - jnp.mean(scaled, axis=-1, keepdims=True)
        - normed * jnp.mean(scaled * normed, axis=-1, keepdims=True)
    )


def edge_forward(source, dest_proj, sender, target, live_count, out_weight, mesh_count):
    preact = source[sender] + dest_proj[target]
    hidden = jax.nn.silu(preact).astype(jnp.bfloat16)
    message = jnp.dot(hidden, out_weight, preferred_element_type=jnp.float32).astype(jnp.bfloat16)
    live_slots = jnp.arange(sender.shape[0], dtype=jnp.int32) < live_count
    onehot = (
        (target[None, :] == jnp.arange(mesh_count, dtype=jnp.int32)[:, None]) & live_slots[None, :]
    ).astype(jnp.bfloat16)
    gathered = jnp.dot(onehot, message, preferred_element_type=jnp.float32)
    return (gathered, preact, onehot, live_slots)


def edge_backward(
    grad_gathered, preact, onehot, live_slots, sender, target, out_weight, table_rows
):
    grad_message = jnp.where(live_slots[:, None], grad_gathered[target], 0.0).astype(jnp.bfloat16)
    grad_hidden = jnp.dot(grad_message, out_weight.T, preferred_element_type=jnp.float32)
    grad_preact = (grad_hidden * silu_slope(preact)).astype(jnp.bfloat16)
    chooser = (sender[None, :] == jnp.arange(table_rows, dtype=jnp.int32)[:, None]).astype(
        jnp.bfloat16
    )
    grad_source = jnp.dot(chooser, grad_preact, preferred_element_type=jnp.float32)
    grad_dest = jnp.dot(onehot, grad_preact, preferred_element_type=jnp.float32)
    return (grad_source, grad_dest)


def encoder_pass(
    extended,
    mesh_rows,
    sender,
    target,
    live_count,
    source_weight,
    dest_weight,
    out_weight,
    norm_gain,
):
    source = jnp.dot(extended, source_weight, preferred_element_type=jnp.float32)
    dest_proj = jnp.dot(mesh_rows, dest_weight, preferred_element_type=jnp.float32)
    gathered, preact, onehot, live_slots = edge_forward(
        source, dest_proj, sender, target, live_count, out_weight, mesh_rows.shape[0]
    )
    shifted, normed, inverse = norm_forward(gathered, norm_gain)
    updated = (mesh_rows.astype(jnp.float32) + shifted).astype(jnp.bfloat16)
    return (updated, (preact, onehot, live_slots, normed, inverse))


def encoder_backward(
    grad_updated, stored, table_rows, sender, target, dest_weight, out_weight, norm_gain
):
    preact, onehot, live_slots, normed, inverse = stored
    grad_gathered = norm_backward(grad_updated, normed, inverse, norm_gain)
    grad_source, grad_dest = edge_backward(
        grad_gathered, preact, onehot, live_slots, sender, target, out_weight, table_rows
    )
    mesh_grad = grad_updated + jnp.dot(
        grad_dest.astype(jnp.bfloat16), dest_weight.T, preferred_element_type=jnp.float32
    )
    return (mesh_grad, grad_source.astype(jnp.bfloat16))


def process_grads(
    updated,
    coarse_proj,
    sender,
    target,
    live_count,
    cotangent,
    source_weight,
    dest_weight,
    out_weight,
    norm_gain,
):
    local_proj = jnp.dot(updated, source_weight, preferred_element_type=jnp.float32)
    source = jnp.concatenate([local_proj, coarse_proj], axis=0)
    dest_proj = jnp.dot(updated, dest_weight, preferred_element_type=jnp.float32)
    gathered, preact, onehot, live_slots = edge_forward(
        source, dest_proj, sender, target, live_count, out_weight, updated.shape[0]
    )
    unused, normed, inverse = norm_forward(gathered, norm_gain)
    grad_out = cotangent.astype(jnp.float32)
    grad_gathered = norm_backward(grad_out, normed, inverse, norm_gain)
    grad_source, grad_dest = edge_backward(
        grad_gathered, preact, onehot, live_slots, sender, target, out_weight, source.shape[0]
    )
    mesh_count = updated.shape[0]
    grad_local = grad_out + jnp.dot(
        grad_source[:mesh_count].astype(jnp.bfloat16),
        source_weight.T,
        preferred_element_type=jnp.float32,
    )
    grad_local = grad_local + jnp.dot(
        grad_dest.astype(jnp.bfloat16), dest_weight.T, preferred_element_type=jnp.float32
    )
    return (grad_local, grad_source[mesh_count:])


def on_device(
    grid_latent,
    mesh_latent,
    cotangent,
    halo_rows,
    encoder_sender,
    encoder_target,
    encoder_count,
    process_sender,
    process_target,
    process_count,
    encoder_source,
    encoder_dest,
    encoder_output,
    encoder_gain,
    process_source,
    process_dest,
    process_output,
    process_gain,
):
    rim_size = halo_rows.shape[0] // 2
    grid_rows = grid_latent.shape[0]
    outgoing = grid_latent[halo_rows]
    padded = padded_2(outgoing, (("patch", 0),), rim_size)
    extended = jnp.concatenate([grid_latent, padded[:rim_size], padded[3 * rim_size :]], axis=0)
    updated, stored = encoder_pass(
        extended,
        mesh_latent,
        encoder_sender,
        encoder_target,
        encoder_count[0],
        encoder_source,
        encoder_dest,
        encoder_output,
        encoder_gain,
    )
    coarse_rows = mesh_latent.shape[0] // 16
    coarse_proj = jnp.dot(
        gathered_copies(updated[:coarse_rows], "group", 0),
        process_source,
        preferred_element_type=jnp.float32,
    )
    grad_local, grad_coarse = process_grads(
        updated,
        coarse_proj,
        process_sender,
        process_target,
        process_count[0],
        cotangent,
        process_source,
        process_dest,
        process_output,
        process_gain,
    )
    back_weight = process_source.astype(jnp.float32).T
    coarse_grad = sum_at_owner(
        jnp.dot(
            grad_coarse,
            back_weight,
            precision=lax.Precision.HIGHEST,
            preferred_element_type=jnp.float32,
        ),
        "group",
        0,
    )
    grad_updated = grad_local.at[:coarse_rows].add(coarse_grad)
    mesh_grad, source_grads = encoder_backward(
        grad_updated,
        stored,
        extended.shape[0],
        encoder_sender,
        encoder_target,
        encoder_dest,
        encoder_output,
        encoder_gain,
    )
    own_grad = jnp.dot(
        source_grads[:grid_rows], encoder_source.T, preferred_element_type=jnp.float32
    )
    returned = padded_2(source_grads[grid_rows:], (("patch", 0),), rim_size)
    peer_sources = jnp.concatenate([returned[:rim_size], returned[3 * rim_size :]], axis=0)
    from_peers = jnp.dot(peer_sources, encoder_source.T, preferred_element_type=jnp.float32)
    grid_grad = own_grad.at[halo_rows].add(from_peers)
    return (grid_grad.astype(jnp.bfloat16), mesh_grad.astype(jnp.bfloat16))


def solution(mesh):
    return jax.shard_map(
        on_device,
        mesh=mesh,
        in_specs=(
            P(("patch", "group"), None),
            P(("patch", "group"), None),
            P(("patch", "group"), None),
            P(("patch", "group")),
            P(("patch", "group")),
            P(("patch", "group")),
            P(("patch", "group")),
            P(("patch", "group")),
            P(("patch", "group")),
            P(("patch", "group")),
            P(),
            P(),
            P(),
            P(),
            P(),
            P(),
            P(),
            P(),
        ),
        out_specs=(P(("patch", "group"), None), P(("patch", "group"), None)),
        check_vma=False,
    )
```

profile of v0, /device:TPU:1, one launch (start us, length us, event | category | flops | bytes accessed | tf_op | source)
XLA Modules:
  0.0 111.0 jit_solution(13511439682962541733)
XLA Ops:
  1.5 2.3 %gather_fusion = bf16[256,512]{1,0:T(8,128)(2,1)S(1)} fusion(bf16[512,512]{1,0:T(8,128)(2,1)} %param.20, s32[1024]{0:T(1024)S(1)} %pad_clamp_fusion.4), kind=kCustom, calls=%fused_computation | custom fusion | bytes 525312 | tf_op jit(solution)/shard_map/gather | solution.py:189
  3.8 4.0 %collective-permute-start = (bf16[128,512]{1,0:T(8,128)(2,1)S(1)}, bf16[128,512]{1,0:T(8,128)(2,1)S(1)}, u32[]{:S(2)}, u32[]{:S(2)}) collective-permute-start(bf16[128,512]{1,0:T(8,128)(2,1)S(1)} %get-tuple-element.20), channel_id=1, source_target_pairs={{0,16},{16,32},{32,48},{48,64},{64,80},{80,96},{96,112},{112,128},... | collective-permute-start | bytes 393224 | tf_op jit(solution)/shard_map/ppermute | solution.py:16
  7.9 6.0 %collective-permute-start.1 = (bf16[128,512]{1,0:T(8,128)(2,1)S(1)}, bf16[128,512]{1,0:T(8,128)(2,1)S(1)}, u32[]{:S(2)}, u32[]{:S(2)}) collective-permute-start(bf16[128,512]{1,0:T(8,128)(2,1)S(1)} %get-tuple-element.21), channel_id=1, source_target_pairs={{16,0},{32,16},{48,32},{64,48},{80,64},{96,80},{112,96},{128,112},... | collective-permute-start | bytes 393224 | tf_op jit(solution)/shard_map/ppermute | solution.py:17
  15.7 3.1 %gather_fusion.2 = f32[768,512]{1,0:T(8,128)} fusion(f32[256,512]{1,0:T(8,128)S(1)} %fusion.69, s32[1024]{0:T(1024)S(1)} %pad_clamp_fusion.2), kind=kCustom, calls=%fused_computation.2 | custom fusion | bytes 3148800 | tf_op jit(solution)/shard_map/gather | solution.py:71
  19.4 3.1 %gather_fusion.1 = f32[768,512]{1,0:T(8,128)} fusion(f32[768,512]{1,0:T(8,128)S(1)} %fusion.7, s32[1024]{0:T(1024)S(1)} %pad_clamp_fusion.3), kind=kCustom, calls=%fused_computation.1 | custom fusion | bytes 3148800 | tf_op jit(solution)/shard_map/gather | solution.py:71
  22.5 2.9 %fusion.67 = (f32[256]{0:T(256)S(1)}, f32[256,512]{1,0:T(8,128)S(1)}) fusion(bf16[512,512]{1,0:T(8,128)(2,1)} %param.32, f32[768,512]{1,0:T(8,128)} %gather_fusion.1, f32[768,512]{1,0:T(8,128)} %gather_fusion.2, s32[768]{0:T(1024)S(1)} %copy-done.15, pred[768]{0:T(1024)(128)(4,1)S(1)} %iota_compare_fusion.9), kind=kOutput, calls=%fused_computation.111 | convolution fusion | flops 607256320 | bytes 4199168 | tf_op jit(solution)/shard_map/dot_general | solution.py:78
  26.5 11.3 %all-to-all-start = ((bf16[16,16,512]{2,1,0:T(8,128)(2,1)}), bf16[16,16,512]{2,1,0:T(8,128)(2,1)S(1)}, u32[]{:S(2)}, u32[]{:S(2)}) async-start(bf16[16,16,512]{2,1,0:T(8,128)(2,1)} %broadcast_in_dim.35), calls=%async_computation | async-start | bytes 524288 | tf_op jit(solution)/shard_map/all_to_all | solution.py:24
  38.1 3.1 %gather_fusion.4 = f32[768,512]{1,0:T(8,128)} fusion(f32[256,512]{1,0:T(8,128)S(1)} %fusion.72, s32[1024]{0:T(1024)S(1)} %pad_clamp_fusion), kind=kCustom, calls=%fused_computation.4 | custom fusion | bytes 3148800 | tf_op jit(solution)/shard_map/gather | solution.py:71
  42.3 7.1 %all-to-all-done = bf16[16,16,512]{2,1,0:T(8,128)(2,1)S(1)} async-done(((bf16[16,16,512]{2,1,0:T(8,128)(2,1)}), bf16[16,16,512]{2,1,0:T(8,128)(2,1)S(1)}, u32[]{:S(2)}, u32[]{:S(2)}) %all-to-all-start) | async-done | bytes 262176 | tf_op jit(solution)/shard_map/all_to_all | solution.py:24
  50.5 3.1 %gather_fusion.3 = f32[768,512]{1,0:T(8,128)} fusion(f32[512,512]{1,0:T(8,128)S(1)} %pad_maximum_fusion, s32[1024]{0:T(1024)S(1)} %pad_clamp_fusion.1), kind=kCustom, calls=%fused_computation.3 | custom fusion | bytes 3148800 | tf_op jit(solution)/shard_map/gather | solution.py:71
  53.6 2.9 %fusion.68 = (f32[256]{0:T(256)S(1)}, f32[256,512]{1,0:T(8,128)S(1)}) fusion(bf16[512,512]{1,0:T(8,128)(2,1)} %param.36, f32[768,512]{1,0:T(8,128)} %gather_fusion.3, f32[768,512]{1,0:T(8,128)} %gather_fusion.4, s32[768]{0:T(1024)S(1)} %copy-done.12, pred[768]{0:T(1024)(128)(4,1)S(1)} %iota_compare_fusion.8), kind=kOutput, calls=%fused_computation.112 | convolution fusion | flops 607256320 | bytes 4199168 | tf_op jit(solution)/shard_map/dot_general | solution.py:78
  57.3 3.3 %gather_fusion.5 = bf16[768,512]{1,0:T(8,128)(2,1)} fusion(bf16[256,512]{1,0:T(8,128)(2,1)S(1)} %fusion.34, s32[1024]{0:T(1024)S(1)} %pad_clamp_fusion), kind=kCustom, calls=%fused_computation.5 | custom fusion | bytes 1575936 | tf_op jit(solution)/shard_map/gather | solution.py:85
  60.6 3.0 %multiply_convert_fusion.1 = bf16[768,512]{1,0:T(8,128)(2,1)S(1)} fusion(bf16[512,512]{1,0:T(8,128)(2,1)S(1)} %copy-done.17, bf16[768,512]{1,0:T(8,128)(2,1)} %gather_fusion.5, pred[768]{0:T(1024)(128)(4,1)S(1)} %iota_compare_fusion.8, f32[768,512]{1,0:T(8,128)} %gather_fusion.3, f32[768,512]{1,0:T(8,128)} %gather_fusion.4), kind=kOutput, calls=%fused_computation.12 | convolution fusion | flops 406978560 | bytes 5243648 | tf_op jit(solution)/shard_map/dot_general | solution.py:86
  65.2 1.4 %fusion.38 = f32[256,512]{1,0:T(8,128)} fusion(bf16[512,512]{1,0:T(8,128)(2,1)S(1)} %copy-done.1, f32[512,512]{1,0:T(8,128)S(1)} %fusion.1), kind=kOutput, calls=%fused_computation.59 | convolution fusion | flops 805306368 | bytes 1572864 | tf_op jit(solution)/shard_map/dot_general | solution.py:223
  66.6 3.7 %all-to-all-start.1 = ((f32[16,16,512]{2,1,0:T(8,128)}), f32[16,16,512]{2,1,0:T(8,128)S(1)}, u32[]{:S(2)}, u32[]{:S(2)}) async-start(f32[16,16,512]{2,1,0:T(8,128)} %bitcast.3), calls=%async_computation.1 | async-start | bytes 1048576 | tf_op jit(solution)/shard_map/all_to_all | solution.py:45
  70.3 1.4 %convolution_add_fusion.2 = f32[256,512]{1,0:T(8,128)S(1)} fusion(bf16[512,512]{1,0:T(8,128)(2,1)S(1)} %copy-done.1, bf16[256,512]{1,0:T(8,128)(2,1)S(1)} %copy-done.3, f32[512,512]{1,0:T(8,128)} %copy-done.6), kind=kOutput, calls=%fused_computation.27 | convolution fusion | flops 134479872 | bytes 1572864 | tf_op jit(solution)/shard_map/dot_general | solution.py:156
  71.7 1.7 %convolution_add_fusion.1 = f32[256,512]{1,0:T(8,128)S(1)} fusion(f32[256,512]{1,0:T(8,128)S(1)} %convolution_add_fusion.2, bf16[512,512]{1,0:T(8,128)(2,1)S(1)} %copy-done.4, bf16[768,512]{1,0:T(8,128)(2,1)} %copy-done.8, s32[768]{0:T(1024)S(1)} %copy-done.12, pred[768]{0:T(1024)(128)(4,1)S(1)} %iota_compare_fusion.8), kind=kOutput, calls=%fused_computation.26 | convolution fusion | flops 336199680 | bytes 2363136 | tf_op jit(solution)/shard_map/dot_general | solution.py:161
  73.4 12.5 %all-to-all-done.1 = f32[16,16,512]{2,1,0:T(8,128)S(1)} async-done(((f32[16,16,512]{2,1,0:T(8,128)}), f32[16,16,512]{2,1,0:T(8,128)S(1)}, u32[]{:S(2)}, u32[]{:S(2)}) %all-to-all-start.1) | async-done | bytes 524320 | tf_op jit(solution)/shard_map/all_to_all | solution.py:45
  86.4 2.7 %gather_fusion.6 = bf16[768,512]{1,0:T(8,128)(2,1)S(1)} fusion(bf16[256,512]{1,0:T(8,128)(2,1)S(1)} %subtract_multiply_fusion, s32[1024]{0:T(1024)S(1)} %pad_clamp_fusion.2), kind=kCustom, calls=%fused_computation.6 | custom fusion | bytes 1575936 | tf_op jit(solution)/shard_map/gather | solution.py:85
  89.2 3.7 %multiply_convert_fusion = bf16[768,512]{1,0:T(8,128)(2,1)} fusion(bf16[512,512]{1,0:T(8,128)(2,1)S(1)} %copy-done.18, bf16[768,512]{1,0:T(8,128)(2,1)S(1)} %gather_fusion.6, pred[768]{0:T(1024)(128)(4,1)S(1)} %iota_compare_fusion.9, f32[768,512]{1,0:T(8,128)} %gather_fusion.1, f32[768,512]{1,0:T(8,128)} %gather_fusion.2), kind=kOutput, calls=%fused_computation.10 | convolution fusion | flops 406978560 | bytes 5243648 | tf_op jit(solution)/shard_map/dot_general | solution.py:86
  92.9 2.5 %fusion.5 = bf16[256,512]{1,0:T(8,128)(2,1)} fusion(f32[256,512]{1,0:T(8,128)S(1)} %fusion.56, bf16[512,512]{1,0:T(8,128)(2,1)S(1)} %copy-done.10, bf16[768,512]{1,0:T(8,128)(2,1)} %multiply_convert_fusion, s32[768]{0:T(1024)S(1)} %copy-done.15, pred[768]{0:T(1024)(128)(4,1)S(1)} %iota_compare_fusion.9), kind=kOutput, calls=%fused_computation.28 | convolution fusion | flops 336330752 | bytes 2100992 | tf_op jit(solution)/shard_map/dot_general | solution.py:125
  96.2 1.9 %collective-permute-start.2 = (bf16[128,512]{1,0:T(8,128)(2,1)S(1)}, bf16[128,512]{1,0:T(8,128)(2,1)S(1)}, u32[]{:S(2)}, u32[]{:S(2)}) collective-permute-start(bf16[128,512]{1,0:T(8,128)(2,1)S(1)} %get-tuple-element.18), channel_id=1, source_target_pairs={{0,16},{16,32},{32,48},{48,64},{64,80},{80,96},{96,112},{112,128},... | collective-permute-start | bytes 393224 | tf_op jit(solution)/shard_map/ppermute | solution.py:16
  98.1 6.7 %collective-permute-start.3 = (bf16[128,512]{1,0:T(8,128)(2,1)S(1)}, bf16[128,512]{1,0:T(8,128)(2,1)S(1)}, u32[]{:S(2)}, u32[]{:S(2)}) collective-permute-start(bf16[128,512]{1,0:T(8,128)(2,1)S(1)} %get-tuple-element.19), channel_id=1, source_target_pairs={{16,0},{32,16},{48,32},{64,48},{80,64},{96,80},{112,96},{128,112},... | collective-permute-start | bytes 393224 | tf_op jit(solution)/shard_map/ppermute | solution.py:17
  107.7 2.5 %scatter_fusion = f32[512,512]{1,0:T(8,128)S(1)} fusion(f32[512,512]{1,0:T(8,128)S(1)} %fusion.36, s32[256]{0:T(256)S(1)} %compare_select_fusion.4, f32[256,512]{1,0:T(8,128)S(1)} %fusion.52), kind=kCustom, calls=%fused_computation.7 | custom fusion | flops 131072 | bytes 1573888 | tf_op jit(solution)/shard_map/scatter-add | solution.py:249
  (87 shorter events, 12.6 us)
Async XLA Ops:
  0.6 18.2 %copy-start = (bf16[512,512]{1,0:T(8,128)(2,1)S(1)}, bf16[512,512]{1,0:T(8,128)(2,1)}, u32[]{:S(2)}) copy-start(bf16[512,512]{1,0:T(8,128)(2,1)} %param.30) | copy-start | bytes 1572868
  0.6 14.5 %copy-start.16 = (s32[768]{0:T(1024)S(1)}, s32[768]{0:T(1024)}, u32[]{:S(2)}) copy-start(s32[768]{0:T(1024)} %param.24) | copy-start | bytes 9220
  0.7 14.6 %copy-start.14 = (s32[768]{0:T(1024)S(1)}, s32[768]{0:T(1024)}, u32[]{:S(2)}) copy-start(s32[768]{0:T(1024)} %param.27) | copy-start | bytes 9220
  0.7 14.6 %copy-start.15 = (s32[768]{0:T(1024)S(1)}, s32[768]{0:T(1024)}, u32[]{:S(2)}) copy-start(s32[768]{0:T(1024)} %param.25) | copy-start | bytes 9220
  0.7 14.6 %copy-start.12 = (s32[768]{0:T(1024)S(1)}, s32[768]{0:T(1024)}, u32[]{:S(2)}) copy-start(s32[768]{0:T(1024)} %param.28) | copy-start | bytes 9220
  0.7 14.6 %copy-start.9 = (bf16[512,512]{1,0:T(8,128)(2,1)S(1)}, bf16[512,512]{1,0:T(8,128)(2,1)}, u32[]{:S(2)}) copy-start(bf16[512,512]{1,0:T(8,128)(2,1)} %param.31) | copy-start | bytes 1572868
  0.7 14.6 %copy-start.7 = (bf16[256,512]{1,0:T(8,128)(2,1)S(1)}, bf16[256,512]{1,0:T(8,128)(2,1)}, u32[]{:S(2)}) copy-start(bf16[256,512]{1,0:T(8,128)(2,1)} %param.21) | copy-start | bytes 786436
  3.8 14.9 %collective-permute-start = (bf16[128,512]{1,0:T(8,128)(2,1)S(1)}, bf16[128,512]{1,0:T(8,128)(2,1)S(1)}, u32[]{:S(2)}, u32[]{:S(2)}) collective-permute-start(bf16[128,512]{1,0:T(8,128)(2,1)S(1)} %get-tuple-element.20), channel_id=1, source_target_pairs={{0,16},{16,32},{32,48},{48,64},{64,80},{80,96},{96,112},{112,128},... | collective-permute-start | bytes 393224 | tf_op jit(solution)/shard_map/ppermute | solution.py:16
  7.9 10.9 %collective-permute-start.1 = (bf16[128,512]{1,0:T(8,128)(2,1)S(1)}, bf16[128,512]{1,0:T(8,128)(2,1)S(1)}, u32[]{:S(2)}, u32[]{:S(2)}) collective-permute-start(bf16[128,512]{1,0:T(8,128)(2,1)S(1)} %get-tuple-element.21), channel_id=1, source_target_pairs={{16,0},{32,16},{48,32},{64,48},{80,64},{96,80},{112,96},{128,112},... | collective-permute-start | bytes 393224 | tf_op jit(solution)/shard_map/ppermute | solution.py:17
  15.7 3.2 %copy-start.2 = (bf16[512,512]{1,0:T(8,128)(2,1)S(1)}, bf16[512,512]{1,0:T(8,128)(2,1)}, u32[]{:S(2)}) copy-start(bf16[512,512]{1,0:T(8,128)(2,1)} %param.20) | copy-start | bytes 1572868
  22.5 3.1 %copy-start.11 = (f32[512]{0:T(512)S(1)}, f32[512]{0:T(512)}, u32[]{:S(2)}) copy-start(f32[512]{0:T(512)} %param.33) | copy-start | bytes 6148
  25.4 12.5 %copy-start.4 = (bf16[512,512]{1,0:T(8,128)(2,1)S(1)}, bf16[512,512]{1,0:T(8,128)(2,1)}, u32[]{:S(2)}) copy-start(bf16[512,512]{1,0:T(8,128)(2,1)} %param.35) | copy-start | bytes 1572868
  26.5 22.9 %all-to-all-start = ((bf16[16,16,512]{2,1,0:T(8,128)(2,1)}), bf16[16,16,512]{2,1,0:T(8,128)(2,1)S(1)}, u32[]{:S(2)}, u32[]{:S(2)}) async-start(bf16[16,16,512]{2,1,0:T(8,128)(2,1)} %broadcast_in_dim.35), calls=%async_computation | async-start | bytes 524288 | tf_op jit(solution)/shard_map/all_to_all | solution.py:24
  38.1 3.1 %copy-start.1 = (bf16[512,512]{1,0:T(8,128)(2,1)S(1)}, bf16[512,512]{1,0:T(8,128)(2,1)}, u32[]{:S(2)}) copy-start(bf16[512,512]{1,0:T(8,128)(2,1)} %param.34) | copy-start | bytes 1572868
  53.6 3.2 %copy-start.3 = (bf16[256,512]{1,0:T(8,128)(2,1)S(1)}, bf16[256,512]{1,0:T(8,128)(2,1)}, u32[]{:S(2)}) copy-start(bf16[256,512]{1,0:T(8,128)(2,1)} %param.22) | copy-start | bytes 786436
  53.6 3.2 %copy-start.13 = (f32[512]{0:T(512)S(1)}, f32[512]{0:T(512)}, u32[]{:S(2)}) copy-start(f32[512]{0:T(512)} %param.37) | copy-start | bytes 6148
  57.3 3.3 %copy-start.17 = (bf16[512,512]{1,0:T(8,128)(2,1)S(1)}, bf16[512,512]{1,0:T(8,128)(2,1)}, u32[]{:S(2)}) copy-start(bf16[512,512]{1,0:T(8,128)(2,1)} %param.36) | copy-start | bytes 1572868
  63.7 3.0 %copy-start.8 = (bf16[768,512]{1,0:T(8,128)(2,1)}, bf16[768,512]{1,0:T(8,128)(2,1)S(1)}, u32[]{:S(2)}) copy-start(bf16[768,512]{1,0:T(8,128)(2,1)S(1)} %multiply_convert_fusion.1) | copy-start | bytes 2359300
  66.6 19.3 %all-to-all-start.1 = ((f32[16,16,512]{2,1,0:T(8,128)}), f32[16,16,512]{2,1,0:T(8,128)S(1)}, u32[]{:S(2)}, u32[]{:S(2)}) async-start(f32[16,16,512]{2,1,0:T(8,128)} %bitcast.3), calls=%async_computation.1 | async-start | bytes 1048576 | tf_op jit(solution)/shard_map/all_to_all | solution.py:45
  86.4 2.7 %copy-start.18 = (bf16[512,512]{1,0:T(8,128)(2,1)S(1)}, bf16[512,512]{1,0:T(8,128)(2,1)}, u32[]{:S(2)}) copy-start(bf16[512,512]{1,0:T(8,128)(2,1)} %param.32) | copy-start | bytes 1572868
  89.1 3.7 %copy-start.10 = (bf16[512,512]{1,0:T(8,128)(2,1)S(1)}, bf16[512,512]{1,0:T(8,128)(2,1)}, u32[]{:S(2)}) copy-start(bf16[512,512]{1,0:T(8,128)(2,1)} %param.31) | copy-start | bytes 1572868
  92.9 2.5 %copy-start.19 = (bf16[768,512]{1,0:T(8,128)(2,1)S(1)}, bf16[768,512]{1,0:T(8,128)(2,1)}, u32[]{:S(2)}) copy-start(bf16[768,512]{1,0:T(8,128)(2,1)} %multiply_convert_fusion) | copy-start | bytes 2359300
  96.2 10.2 %collective-permute-start.2 = (bf16[128,512]{1,0:T(8,128)(2,1)S(1)}, bf16[128,512]{1,0:T(8,128)(2,1)S(1)}, u32[]{:S(2)}, u32[]{:S(2)}) collective-permute-start(bf16[128,512]{1,0:T(8,128)(2,1)S(1)} %get-tuple-element.18), channel_id=1, source_target_pairs={{0,16},{16,32},{32,48},{48,64},{64,80},{80,96},{96,112},{112,128},... | collective-permute-start | bytes 393224 | tf_op jit(solution)/shard_map/ppermute | solution.py:16
  98.1 9.2 %collective-permute-start.3 = (bf16[128,512]{1,0:T(8,128)(2,1)S(1)}, bf16[128,512]{1,0:T(8,128)(2,1)S(1)}, u32[]{:S(2)}, u32[]{:S(2)}) collective-permute-start(bf16[128,512]{1,0:T(8,128)(2,1)S(1)} %get-tuple-element.19), channel_id=1, source_target_pairs={{16,0},{32,16},{48,32},{64,48},{80,64},{96,80},{112,96},{128,112},... | collective-permute-start | bytes 393224 | tf_op jit(solution)/shard_map/ppermute | solution.py:17
  (2 other events, 2.0 us)
where the time goes:
time: 112 us; the launch traced here: 111 us
  starting transfers between devices  33.6 us (30%)
  matrix products  24.2 us (22%)
  local copies, waits for them, and re-layouts  23.3 us (21%)
  waiting for transfers between devices  21.6 us (19%)
  other arithmetic  5.81 us (5%)
  between operations  2.49 us (2%)
    ppermute x2, starting transfers between devices, padded_2(): after = lax.ppermute(initial, axis, down)  12.7 us
    all_to_all x1, waiting for transfers between devices, sum_at_owner(): parts = lax.all_to_all(cut_along(x, dim, length), axis, 0, 0, tiled=True)  12.5 us
    gather x4, local copies, waits for them, and re-layouts, edge_forward(): preact = source[sender] + dest_proj[target]  12.4 us
    all_to_all x1, starting transfers between devices, from_everyone(): return lax.all_to_all(copies, axis, split_axis=0, concat_axis=0, tiled=True)  11.3 us
    all_to_all x1, waiting for transfers between devices, from_everyone(): return lax.all_to_all(copies, axis, split_axis=0, concat_axis=0, tiled=True)  7.07 us
    dot_general x2, matrix products, edge_backward(): jnp.dot(grad_message, out_weight.T, preferred_element_type=jnp.float32)  6.75 us
    gather x2, local copies, waits for them, and re-layouts, edge_backward(): grad_gathered[target]  6.01 us
    ppermute x2, starting transfers between devices, padded_2(): before = lax.ppermute(last, axis, up)  5.94 us
  transfers between devices with their start and end apart: 6, of which 4 were waited for; matrix products, arithmetic and copies ran while one was open for 10% of the time, Pallas kernels for 0%

commit v1 on v0

v1 whole, which is shorter than its diff:
```python
import functools

import jax
import jax.numpy as jnp
from jax import lax
from jax.experimental import pallas as pl
from jax.experimental.pallas import tpu as pltpu
from jax.sharding import PartitionSpec as P

EPSILON = 1e-05
F32 = jnp.float32
BF16 = jnp.bfloat16
COARSE = 16
LANES = 128


def mm(a, b):
    return jnp.dot(a, b, preferred_element_type=F32)


def mm_t(a, b):
    return lax.dot_general(a, b, (((1,), (1,)), ((), ())), preferred_element_type=F32)


def column(row):
    return jnp.transpose(jnp.broadcast_to(row, (LANES, row.shape[1])))


def onehot_cols(ref, col, start, stop, shift):
    lane = lax.broadcasted_iota(jnp.int32, (col.shape[0], LANES), 1)
    for c in range(start, stop, LANES):
        width = min(LANES, stop - c)
        hit = jnp.where(col == lane + (c - shift), 1.0, 0.0).astype(BF16)
        ref[:, c : c + width] = hit[:, :width]


def onehot_rows(ref, row, start, stop, shift):
    for c in range(start, stop, LANES):
        height = min(LANES, stop - c)
        sub = lax.broadcasted_iota(jnp.int32, (height, row.shape[1]), 0)
        hit = jnp.where(row == sub + (c - shift), 1.0, 0.0).astype(BF16)
        ref[c : c + height, :] = hit


def norm_backward(scaled, normed, inverse):
    first = jnp.mean(scaled, axis=-1, keepdims=True)
    second = jnp.mean(scaled * normed, axis=-1, keepdims=True)
    return inverse * (scaled - first - normed * second)


def norm_forward(values):
    center = values - jnp.mean(values, axis=-1, keepdims=True)
    inverse = lax.rsqrt(jnp.mean(center * center, axis=-1, keepdims=True) + EPSILON)
    return center * inverse, inverse


def silu_pair(values):
    logistic = 0.5 * jnp.tanh(0.5 * values) + 0.5
    hidden = values * logistic
    return hidden, logistic + hidden * (1.0 - logistic)


def kernel(
    n_patch,
    n_group,
    grid_hbm,
    mesh_hbm,
    cot_hbm,
    w_src_hbm,
    w_dst_hbm,
    w_out_hbm,
    p_src_hbm,
    p_dst_hbm,
    p_out_hbm,
    halo_ref,
    e_send_ref,
    e_targ_ref,
    e_count_ref,
    p_send_ref,
    p_targ_ref,
    p_count_ref,
    e_gain_ref,
    p_gain_ref,
    grid_out,
    mesh_out,
    ext,
    mesh_v,
    cot_v,
    w_src,
    w_dst,
    w_out,
    p_src,
    p_dst,
    p_out,
    outgoing,
    hot_h,
    hot_ht,
    hot1,
    hot1t,
    hot2,
    hot2t,
    tbl1,
    tbl2,
    coarse,
    acc,
    slope1,
    slope2,
    hid,
    gpre,
    normed,
    inv,
    gup,
    gnode,
    gnode16,
    gcoarse,
    rs_buf,
    g_halo,
    peers,
    own,
    load_sem,
    halo_send,
    halo_recv,
    co_send,
    co_recv,
    rs_send,
    rs_recv,
    back_send,
    back_recv,
):
    patch, group = lax.axis_index("patch"), lax.axis_index("group")
    after = lax.rem(patch + 1, n_patch)
    before = lax.rem(patch + n_patch - 1, n_patch)
    grid_rows, mesh_rows = grid_hbm.shape[0], mesh_hbm.shape[0]
    rim = outgoing.shape[0] // 2
    slots = e_send_ref.shape[1]
    chunk = 256
    mesh_id = pl.DeviceIdType.MESH

    loads = []
    pairs = (
        (grid_hbm, ext.at[0:grid_rows]),
        (w_src_hbm, w_src),
        (mesh_hbm, mesh_v),
        (w_dst_hbm, w_dst),
        (w_out_hbm, w_out),
        (p_src_hbm, p_src),
        (p_dst_hbm, p_dst),
        (p_out_hbm, p_out),
        (cot_hbm, cot_v),
    )
    for n, (src, dst) in enumerate(pairs):
        copy = pltpu.make_async_copy(src, dst, load_sem.at[n])
        copy.start()
        loads.append(copy)

    barrier = pltpu.get_barrier_semaphore()
    for neighbour in (before, after):
        pl.semaphore_signal(
            barrier, inc=1, device_id={"patch": neighbour}, device_id_type=mesh_id
        )

    def greet(k, carry):
        peer = lax.rem(group + k, n_group)
        pl.semaphore_signal(barrier, inc=1, device_id={"group": peer}, device_id_type=mesh_id)
        return carry

    lax.fori_loop(1, n_group, greet, 0)

    halo_row = halo_ref[...]
    onehot_cols(hot_h, column(halo_row), 0, grid_rows, 0)
    loads[0].wait()
    outgoing[...] = mm(hot_h[...], ext[0:grid_rows, :]).astype(BF16)
    pl.semaphore_wait(barrier, n_group + 1)

    def remote(src, dst, send, recv, where):
        return pltpu.make_async_remote_copy(
            src_ref=src,
            dst_ref=dst,
            send_sem=send,
            recv_sem=recv,
            device_id=where,
            device_id_type=mesh_id,
        )

    up = remote(
        outgoing.at[rim : 2 * rim],
        ext.at[grid_rows : grid_rows + rim],
        halo_send.at[0],
        halo_recv.at[0],
        {"patch": after},
    )
    down = remote(
        outgoing.at[0:rim],
        ext.at[grid_rows + rim : grid_rows + 2 * rim],
        halo_send.at[1],
        halo_recv.at[1],
        {"patch": before},
    )
    up.start()
    down.start()

    slot = lax.broadcasted_iota(jnp.int32, (1, slots), 1)
    own1 = grid_rows + mesh_rows
    sender = e_send_ref[...]
    sender = jnp.where(sender >= grid_rows, sender + mesh_rows, sender)
    target = jnp.where(slot < e_count_ref[0], e_targ_ref[...], -1)
    sender_col, target_col = column(sender), column(target)
    onehot_cols(hot1, sender_col, 0, grid_rows, 0)
    onehot_cols(hot1, target_col, grid_rows, own1, grid_rows)
    onehot_cols(hot1, sender_col, own1, own1 + 2 * rim, 0)
    loads[1].wait()
    tbl1[0:grid_rows, :] = mm(ext[0:grid_rows, :], w_src[...]).astype(BF16)
    loads[2].wait()
    loads[3].wait()
    tbl1[grid_rows:own1, :] = mm(mesh_v[...], w_dst[...]).astype(BF16)

    def chunks(body):
        def step(i, carry):
            body(pl.ds(pl.multiple_of(i * chunk, chunk), chunk))
            return carry

        lax.fori_loop(0, slots // chunk, step, 0)

    def early1(rows):
        acc[rows, :] = mm(hot1[rows, 0:own1], tbl1[0:own1, :])

    chunks(early1)
    onehot_rows(hot1t, sender, 0, grid_rows, 0)
    onehot_rows(hot1t, target, grid_rows, own1, grid_rows)
    onehot_rows(hot1t, sender, own1, own1 + 2 * rim, 0)
    p_sender = p_send_ref[...]
    p_sender = jnp.where(p_sender >= mesh_rows, p_sender + mesh_rows, p_sender)
    p_target = jnp.where(slot < p_count_ref[0], p_targ_ref[...], -1)
    p_sender_col, p_target_col = column(p_sender), column(p_target)
    local2 = 2 * mesh_rows
    all2 = local2 + coarse.shape[0]
    onehot_cols(hot2, p_sender_col, 0, mesh_rows, 0)
    onehot_cols(hot2, p_target_col, mesh_rows, local2, mesh_rows)
    onehot_cols(hot2, p_sender_col, local2, all2, 0)
    onehot_rows(hot2t, p_sender, 0, mesh_rows, 0)
    onehot_rows(hot2t, p_target, mesh_rows, local2, mesh_rows)
    onehot_rows(hot2t, p_sender, local2, all2, 0)
    onehot_rows(hot_ht, halo_row, 0, grid_rows, 0)

    up.wait()
    down.wait()
    tbl1[own1 : own1 + 2 * rim, :] = mm(ext[grid_rows : grid_rows + 2 * rim, :], w_src[...]).astype(
        BF16
    )

    def late1(rows):
        preact = acc[rows, :] + mm(hot1[rows, own1 : own1 + 2 * rim], tbl1[own1 : own1 + 2 * rim, :])
        hidden, slope = silu_pair(preact)
        hid[rows, :] = hidden.astype(BF16)
        slope1[rows, :] = slope

    chunks(late1)
    for n in range(4, len(pairs)):
        loads[n].wait()
    summed = mm(hot1t[grid_rows:own1, :], hid[...]).astype(BF16)
    normed1, inverse1 = norm_forward(mm(summed, w_out[...]))
    normed[...] = normed1
    inv[...] = jnp.broadcast_to(inverse1, inv.shape)
    updated = (mesh_v[...].astype(F32) + normed1 * e_gain_ref[...]).astype(BF16)
    projected = mm(updated, p_src[...]).astype(BF16)
    tbl2[0:mesh_rows, :] = projected
    own_rows = pl.ds(pl.multiple_of(group * COARSE, COARSE), COARSE)

    def coarse_copy(k):
        return remote(
            tbl2.at[0:COARSE],
            coarse.at[own_rows],
            co_send.at[k - 1],
            co_recv.at[k - 1],
            {"group": lax.rem(group + k, n_group)},
        )

    def each_peer(body):
        def step(k, carry):
            body(k)
            return carry

        lax.fori_loop(1, n_group, step, 0)

    each_peer(lambda k: coarse_copy(k).start())
    coarse[own_rows, :] = projected[0:COARSE, :]
    tbl2[mesh_rows:local2, :] = mm(updated, p_dst[...]).astype(BF16)

    def early2(rows):
        acc[rows, :] = mm(hot2[rows, 0:local2], tbl2[...])

    chunks(early2)
    each_peer(lambda k: coarse_copy(k).wait())

    def late2(rows):
        preact = acc[rows, :] + mm(hot2[rows, local2:all2], coarse[...])
        hidden, slope = silu_pair(preact)
        hid[rows, :] = hidden.astype(BF16)
        slope2[rows, :] = slope

    chunks(late2)
    summed2 = mm(hot2t[mesh_rows:local2, :], hid[...]).astype(BF16)
    normed2, inverse2 = norm_forward(mm(summed2, p_out[...]))
    cot = cot_v[...].astype(F32)
    node2 = norm_backward(cot * p_gain_ref[...], normed2, inverse2).astype(BF16)
    gnode[...] = mm_t(node2, p_out[...]).astype(BF16)

    def back2(rows):
        grad = mm(hot2[rows, mesh_rows:local2], gnode[...])
        gpre[rows, :] = (grad * slope2[rows, :]).astype(BF16)

    chunks(back2)
    gcoarse[...] = mm(hot2t[local2:all2, :], gpre[...]).astype(BF16)

    def rs_copy(k):
        peer = lax.rem(group + k, n_group)
        return remote(
            gcoarse.at[pl.ds(pl.multiple_of(peer * COARSE, COARSE), COARSE)],
            rs_buf.at[k - 1],
            rs_send.at[k - 1],
            rs_recv.at[k - 1],
            {"group": peer},
        )

    each_peer(lambda k: rs_copy(k).start())
    g_local = mm(hot2t[0:mesh_rows, :], gpre[...]).astype(BF16)
    g_dest = mm(hot2t[mesh_rows:local2, :], gpre[...]).astype(BF16)
    grad_up = cot + mm_t(g_local, p_src[...]) + mm_t(g_dest, p_dst[...])
    gup[...] = grad_up
    gain = e_gain_ref[...]
    node1 = norm_backward(grad_up * gain, normed[...], inv[:, 0:1])
    row = lax.broadcasted_iota(jnp.int32, node1.shape, 0)
    node1 = jnp.where(row < COARSE, 0.0, node1).astype(BF16)
    gnode[...] = mm_t(node1, w_out[...]).astype(BF16)

    def early3(rows):
        acc[rows, :] = mm(hot1[rows, grid_rows:own1], gnode[...])

    chunks(early3)
    gnode16[...] = jnp.zeros_like(gnode16)
    each_peer(lambda k: rs_copy(k).wait())

    total = gcoarse[own_rows, :].astype(F32)
    for k in range(n_group - 1):
        total = total + rs_buf[k].astype(F32)
    high = total.astype(BF16)
    low = (total - high.astype(F32)).astype(BF16)
    both = mm_t(jnp.concatenate([high, low], axis=0), p_src[...])
    fixed = gup[0:COARSE, :] + both[0:COARSE, :] + both[COARSE:, :]
    gup[0:COARSE, :] = fixed
    node16 = norm_backward(fixed * gain, normed[0:COARSE, :], inv[0:COARSE, 0:1]).astype(BF16)
    gnode16[0:COARSE, :] = mm_t(node16, w_out[...]).astype(BF16)

    def late3(rows):
        grad = acc[rows, :] + mm(hot1[rows, grid_rows : grid_rows + LANES], gnode16[...])
        gpre[rows, :] = (grad * slope1[rows, :]).astype(BF16)

    chunks(late3)
    g_halo[...] = mm(hot1t[own1 : own1 + 2 * rim, :], gpre[...]).astype(BF16)
    back_up = remote(
        g_halo.at[rim : 2 * rim],
        peers.at[0:rim],
        back_send.at[0],
        back_recv.at[0],
        {"patch": after},
    )
    back_down = remote(
        g_halo.at[0:rim],
        peers.at[rim : 2 * rim],
        back_send.at[1],
        back_recv.at[1],
        {"patch": before},
    )
    back_up.start()
    back_down.start()
    g_own = mm(hot1t[0:grid_rows, :], gpre[...]).astype(BF16)
    own[...] = mm_t(g_own, w_src[...])
    g_targ = mm(hot1t[grid_rows:own1, :], gpre[...]).astype(BF16)
    mesh_out[...] = (gup[...] + mm_t(g_targ, w_dst[...])).astype(BF16)
    back_up.wait()
    back_down.wait()
    returned = mm_t(peers[...], w_src[...]).astype(BF16)
    grid_out[...] = (own[...] + mm(hot_ht[...], returned)).astype(BF16)


def on_device(
    n_patch,
    n_group,
    grid_latent,
    mesh_latent,
    cotangent,
    halo_rows,
    encoder_sender,
    encoder_target,
    encoder_count,
    process_sender,
    process_target,
    process_count,
    encoder_source,
    encoder_dest,
    encoder_output,
    encoder_gain,
    process_source,
    process_dest,
    process_output,
    process_gain,
):
    g, d = grid_latent.shape
    m = mesh_latent.shape[0]
    h2 = halo_rows.shape[0]
    e = encoder_sender.shape[0]
    nc = n_group * COARSE
    hbm = pl.BlockSpec(memory_space=pl.ANY)
    vmem = pl.BlockSpec(memory_space=pltpu.VMEM)
    smem = pl.BlockSpec(memory_space=pltpu.SMEM)
    dma = pltpu.SemaphoreType.DMA
    out = pl.pallas_call(
        functools.partial(kernel, n_patch, n_group),
        out_shape=(
            jax.ShapeDtypeStruct((g, d), BF16),
            jax.ShapeDtypeStruct((m, d), BF16),
        ),
        in_specs=[hbm] * 9 + [vmem, vmem, vmem, smem, vmem, vmem, smem, vmem, vmem],
        out_specs=(vmem, vmem),
        scratch_shapes=[
            pltpu.VMEM((g + h2, d), BF16),
            pltpu.VMEM((m, d), BF16),
            pltpu.VMEM((m, d), BF16),
        ]
        + [pltpu.VMEM((d, d), BF16)] * 6
        + [
            pltpu.VMEM((h2, d), BF16),
            pltpu.VMEM((h2, g), BF16),
            pltpu.VMEM((g, h2), BF16),
            pltpu.VMEM((e, g + m + h2), BF16),
            pltpu.VMEM((g + m + h2, e), BF16),
            pltpu.VMEM((e, 2 * m + nc), BF16),
            pltpu.VMEM((2 * m + nc, e), BF16),
            pltpu.VMEM((g + m + h2, d), BF16),
            pltpu.VMEM((2 * m, d), BF16),
            pltpu.VMEM((nc, d), BF16),
            pltpu.VMEM((e, d), F32),
            pltpu.VMEM((e, d), F32),
            pltpu.VMEM((e, d), F32),
            pltpu.VMEM((e, d), BF16),
            pltpu.VMEM((e, d), BF16),
            pltpu.VMEM((m, d), F32),
            pltpu.VMEM((m, LANES), F32),
            pltpu.VMEM((m, d), F32),
            pltpu.VMEM((m, d), BF16),
            pltpu.VMEM((LANES, d), BF16),
            pltpu.VMEM((nc, d), BF16),
            pltpu.VMEM((n_group - 1, COARSE, d), BF16),
            pltpu.VMEM((h2, d), BF16),
            pltpu.VMEM((h2, d), BF16),
            pltpu.VMEM((g, d), F32),
            dma((9,)),
            dma((2,)),
            dma((2,)),
            dma((n_group - 1,)),
            dma((n_group - 1,)),
            dma((n_group - 1,)),
            dma((n_group - 1,)),
            dma((2,)),
            dma((2,)),
        ],
        compiler_params=pltpu.CompilerParams(
            collective_id=0, has_side_effects=True, vmem_limit_bytes=40 * 1024 * 1024
        ),
        name="step",
    )(
        grid_latent,
        mesh_latent,
        cotangent,
        encoder_source,
        encoder_dest,
        encoder_output,
        process_source,
        process_dest,
        process_output,
        halo_rows.reshape(1, h2),
        encoder_sender.reshape(1, e),
        encoder_target.reshape(1, e),
        encoder_count,
        process_sender.reshape(1, e),
        process_target.reshape(1, e),
        process_count,
        encoder_gain.reshape(1, d),
        process_gain.reshape(1, d),
    )
    return out


def solution(mesh):
    both = P(("patch", "group"))
    rows = P(("patch", "group"), None)
    return jax.shard_map(
        functools.partial(on_device, mesh.shape["patch"], mesh.shape["group"]),
        mesh=mesh,
        in_specs=(rows,) * 3 + (both,) * 7 + (P(),) * 8,
        out_specs=(rows, rows),
        check_vma=False,
    )
```

time: 112 us -> 66.9 us (0.60)
  Pallas kernels: 0 us -> 50.8 us
  starting transfers between devices: 33.6 us -> 0 us
  matrix products: 24.2 us -> 0 us
  waiting for transfers between devices: 21.6 us -> 0 us
  local copies, waits for them, and re-layouts: 23.3 us -> 13.4 us
  other arithmetic: 5.81 us -> 0 us
    pallas_call x0 -> x1, Pallas kernels: none -> 50.8 us  [on_device(): pl.pallas_call(functools.partial(kernel, n_patch, n_group), out_shape=(ja...]
    dot_general x17 -> x0, matrix products: 24.2 us -> none  [the longest x2 6.75 us: edge_backward(): jnp.dot(grad_message, out_weight.T, preferred_element_type=jnp.float32)]
    gather x7 -> x0, local copies, waits for them, and re-layouts: 20.8 us -> none  [the longest x4 12.4 us: edge_forward(): preact = source[sender] + dest_proj[target]]
    all_to_all x2 -> x0, waiting for transfers between devices: 19.5 us -> none  [the longest x1 12.5 us: sum_at_owner(): parts = lax.all_to_all(cut_along(x, dim, length), axis, 0, 0, tiled=True)]
    ppermute x4 -> x0, starting transfers between devices: 18.6 us -> none  [the longest x2 12.7 us: padded_2(): after = lax.ppermute(initial, axis, down)]
    all_to_all x2 -> x0, starting transfers between devices: 14.9 us -> none  [the longest x1 11.3 us: from_everyone(): return lax.all_to_all(copies, axis, split_axis=0, concat_axis=0, tiled=True)]
    unnamed x40 -> x34, local copies, waits for them, and re-layouts: 1.81 us -> 13.4 us
    scatter-add x2 -> x0, other arithmetic: 2.5 us -> none  [the longest x1 2.49 us: on_device(): grid_grad = own_grad.at[halo_rows].add(from_peers)]
  transfers between devices with their start and end apart: 6 -> 0, of which waited for: 4 -> 0; matrix products, arithmetic and copies ran while one was open for 10% -> 0% of each run, Pallas kernels for 0% -> 0%
where the time goes in v1:
time: 66.9 us; the launch traced here: 66.3 us
  Pallas kernels  50.8 us (76%)
  local copies, waits for them, and re-layouts  13.4 us (20%)
  between operations  1.99 us (3%)
    pallas_call x1, Pallas kernels, on_device(): pl.pallas_call(functools.partial(kernel, n_patch, n_group), out_shape=(ja...  50.8 us
    unnamed x34, local copies, waits for them, and re-layouts  13.4 us

profile of v1, /device:TPU:1, one launch (start us, length us, event | category | flops | bytes accessed | tf_op | source)
XLA Modules:
  0.0 66.3 jit_solution(8883806304867649145)
XLA Ops:
  1.3 0.0 copy-start.12
  1.9 0.0 copy-start.13
  2.0 0.0 copy-done.12
  2.0 0.7 copy-done.13
  2.6 0.0 copy-start.14
  2.6 0.7 %copy-done.14 = s32[768]{0:T(1024)S(1)} copy-done((s32[768]{0:T(1024)S(1)}, s32[768]{0:T(1024)}, u32[]{:S(2)}) %copy-start.14) | copy-done | bytes 3096
  3.3 0.0 copy-start.15
  3.3 0.7 %copy-done.15 = s32[768]{0:T(1024)S(1)} copy-done((s32[768]{0:T(1024)S(1)}, s32[768]{0:T(1024)}, u32[]{:S(2)}) %copy-start.15) | copy-done | bytes 3096
  4.0 0.0 copy-start.9
  4.0 0.7 %copy-done.9 = f32[512]{0:T(512)S(1)} copy-done((f32[512]{0:T(512)S(1)}, f32[512]{0:T(512)}, u32[]{:S(2)}) %copy-start.9) | copy-done | bytes 2072
  4.7 0.0 copy-done.10
  4.7 0.0 copy-done.11
  4.7 1.0 %copy-done = bf16[512,512]{1,0:T(8,128)(2,1)S(1)} copy-done((bf16[512,512]{1,0:T(8,128)(2,1)S(1)}, bf16[512,512]{1,0:T(8,128)(2,1)}, u32[]{:S(2)}) %copy-start) | copy-done | bytes 524312
  5.8 1.0 %copy-done.1 = bf16[512,512]{1,0:T(8,128)(2,1)S(1)} copy-done((bf16[512,512]{1,0:T(8,128)(2,1)S(1)}, bf16[512,512]{1,0:T(8,128)(2,1)}, u32[]{:S(2)}) %copy-start.1) | copy-done | bytes 524312
  6.8 1.0 %copy-done.2 = bf16[512,512]{1,0:T(8,128)(2,1)S(1)} copy-done((bf16[512,512]{1,0:T(8,128)(2,1)S(1)}, bf16[512,512]{1,0:T(8,128)(2,1)}, u32[]{:S(2)}) %copy-start.2) | copy-done | bytes 524312
  7.8 1.0 %copy-done.3 = bf16[512,512]{1,0:T(8,128)(2,1)S(1)} copy-done((bf16[512,512]{1,0:T(8,128)(2,1)S(1)}, bf16[512,512]{1,0:T(8,128)(2,1)}, u32[]{:S(2)}) %copy-start.3) | copy-done | bytes 524312
  8.9 1.0 %copy-done.4 = bf16[512,512]{1,0:T(8,128)(2,1)S(1)} copy-done((bf16[512,512]{1,0:T(8,128)(2,1)S(1)}, bf16[512,512]{1,0:T(8,128)(2,1)}, u32[]{:S(2)}) %copy-start.4) | copy-done | bytes 524312
  9.9 1.0 %copy-done.5 = bf16[512,512]{1,0:T(8,128)(2,1)S(1)} copy-done((bf16[512,512]{1,0:T(8,128)(2,1)S(1)}, bf16[512,512]{1,0:T(8,128)(2,1)}, u32[]{:S(2)}) %copy-start.5) | copy-done | bytes 524312
  11.0 1.0 %copy-done.6 = bf16[512,512]{1,0:T(8,128)(2,1)S(1)} copy-done((bf16[512,512]{1,0:T(8,128)(2,1)S(1)}, bf16[512,512]{1,0:T(8,128)(2,1)}, u32[]{:S(2)}) %copy-start.6) | copy-done | bytes 524312
  12.0 0.9 %copy-done.7 = bf16[256,512]{1,0:T(8,128)(2,1)S(1)} copy-done((bf16[256,512]{1,0:T(8,128)(2,1)S(1)}, bf16[256,512]{1,0:T(8,128)(2,1)}, u32[]{:S(2)}) %copy-start.7) | copy-done | bytes 262168
  13.0 0.9 %copy-done.8 = bf16[256,512]{1,0:T(8,128)(2,1)S(1)} copy-done((bf16[256,512]{1,0:T(8,128)(2,1)S(1)}, bf16[256,512]{1,0:T(8,128)(2,1)}, u32[]{:S(2)}) %copy-start.8) | copy-done | bytes 262168
  13.9 50.8 %step.1 = (bf16[512,512]{1,0:T(8,128)(2,1)S(1)}, bf16[256,512]{1,0:T(8,128)(2,1)S(1)}) custom-call(bf16[512,512]{1,0:T(8,128)(2,1)S(1)} %copy-done, bf16[256,512]{1,0:T(8,128)(2,1)S(1)} %copy-done.7, bf16[256,512]{1,0:T(8,128)(2,1)S(1)} %copy-done.8, bf16[512,512]{1,0:T(8,128)(2,1)S(1)} %copy-done.1, bf16[512,512]{1,0:T(8,128)(2,1)S(1)} %copy-done.2, ...), custom_call_target="tpu_custom_call" | custom-call | tf_op jit(solution)/shard_map/step/pallas_call | solution.py:417
  64.8 0.8 %copy.24 = bf16[512,512]{1,0:T(8,128)(2,1)} copy(bf16[512,512]{1,0:T(8,128)(2,1)S(1)} %get-tuple-element.4) | data formatting | bytes 1048576
  65.6 0.7 %copy.25 = bf16[256,512]{1,0:T(8,128)(2,1)} copy(bf16[256,512]{1,0:T(8,128)(2,1)S(1)} %get-tuple-element.5) | data formatting | bytes 524288
  (15 shorter events, 0.0 us)
Async XLA Ops:
  1.3 0.7 %copy-start.12 = (s32[768]{0:T(1024)S(1)}, s32[768]{0:T(1024)}, u32[]{:S(2)}) copy-start(s32[768]{0:T(1024)} %param.22) | copy-start | bytes 9220
  1.9 0.7 %copy-start.13 = (s32[768]{0:T(1024)S(1)}, s32[768]{0:T(1024)}, u32[]{:S(2)}) copy-start(s32[768]{0:T(1024)} %param.23) | copy-start | bytes 9220
  2.6 0.7 %copy-start.14 = (s32[768]{0:T(1024)S(1)}, s32[768]{0:T(1024)}, u32[]{:S(2)}) copy-start(s32[768]{0:T(1024)} %param.25) | copy-start | bytes 9220
  3.3 0.7 %copy-start.15 = (s32[768]{0:T(1024)S(1)}, s32[768]{0:T(1024)}, u32[]{:S(2)}) copy-start(s32[768]{0:T(1024)} %param.26) | copy-start | bytes 9220
  4.0 0.7 %copy-start.9 = (f32[512]{0:T(512)S(1)}, f32[512]{0:T(512)}, u32[]{:S(2)}) copy-start(f32[512]{0:T(512)} %param.31) | copy-start | bytes 6148
  4.0 0.7 %copy-start.10 = (f32[512]{0:T(512)S(1)}, f32[512]{0:T(512)}, u32[]{:S(2)}) copy-start(f32[512]{0:T(512)} %param.35) | copy-start | bytes 6148
  4.0 0.7 %copy-start.11 = (s32[256]{0:T(256)S(1)}, s32[256]{0:T(256)}, u32[]{:S(2)}) copy-start(s32[256]{0:T(256)} %param.21) | copy-start | bytes 3076
  4.7 1.0 %copy-start = (bf16[512,512]{1,0:T(8,128)(2,1)S(1)}, bf16[512,512]{1,0:T(8,128)(2,1)}, u32[]{:S(2)}) copy-start(bf16[512,512]{1,0:T(8,128)(2,1)} %grid_hbm.1) | copy-start | bytes 1572868
  5.8 1.0 %copy-start.1 = (bf16[512,512]{1,0:T(8,128)(2,1)S(1)}, bf16[512,512]{1,0:T(8,128)(2,1)}, u32[]{:S(2)}) copy-start(bf16[512,512]{1,0:T(8,128)(2,1)} %w_src_hbm.1) | copy-start | bytes 1572868
  6.8 1.0 %copy-start.2 = (bf16[512,512]{1,0:T(8,128)(2,1)S(1)}, bf16[512,512]{1,0:T(8,128)(2,1)}, u32[]{:S(2)}) copy-start(bf16[512,512]{1,0:T(8,128)(2,1)} %w_dst_hbm.1) | copy-start | bytes 1572868
  7.8 1.0 %copy-start.3 = (bf16[512,512]{1,0:T(8,128)(2,1)S(1)}, bf16[512,512]{1,0:T(8,128)(2,1)}, u32[]{:S(2)}) copy-start(bf16[512,512]{1,0:T(8,128)(2,1)} %w_out_hbm.1) | copy-start | bytes 1572868
  8.9 1.0 %copy-start.4 = (bf16[512,512]{1,0:T(8,128)(2,1)S(1)}, bf16[512,512]{1,0:T(8,128)(2,1)}, u32[]{:S(2)}) copy-start(bf16[512,512]{1,0:T(8,128)(2,1)} %p_src_hbm.1) | copy-start | bytes 1572868
  9.9 1.0 %copy-start.5 = (bf16[512,512]{1,0:T(8,128)(2,1)S(1)}, bf16[512,512]{1,0:T(8,128)(2,1)}, u32[]{:S(2)}) copy-start(bf16[512,512]{1,0:T(8,128)(2,1)} %p_dst_hbm.1) | copy-start | bytes 1572868
  11.0 1.0 %copy-start.6 = (bf16[512,512]{1,0:T(8,128)(2,1)S(1)}, bf16[512,512]{1,0:T(8,128)(2,1)}, u32[]{:S(2)}) copy-start(bf16[512,512]{1,0:T(8,128)(2,1)} %p_out_hbm.1) | copy-start | bytes 1572868
  12.0 0.9 %copy-start.7 = (bf16[256,512]{1,0:T(8,128)(2,1)S(1)}, bf16[256,512]{1,0:T(8,128)(2,1)}, u32[]{:S(2)}) copy-start(bf16[256,512]{1,0:T(8,128)(2,1)} %mesh_hbm.1) | copy-start | bytes 786436
  13.0 0.9 %copy-start.8 = (bf16[256,512]{1,0:T(8,128)(2,1)S(1)}, bf16[256,512]{1,0:T(8,128)(2,1)}, u32[]{:S(2)}) copy-start(bf16[256,512]{1,0:T(8,128)(2,1)} %cot_hbm.1) | copy-start | bytes 786436

commit v2 on v1

--- a/solution.py
+++ b/solution.py
@@ -58,6 +58,10 @@
     logistic = 0.5 * jnp.tanh(0.5 * values) + 0.5
     hidden = values * logistic
     return hidden, logistic + hidden * (1.0 - logistic)
+
+
+def silu(values):
+    return values * (0.5 * jnp.tanh(0.5 * values) + 0.5)
 
 
 def kernel(
@@ -72,15 +76,15 @@
     p_src_hbm,
     p_dst_hbm,
     p_out_hbm,
-    halo_ref,
-    e_send_ref,
-    e_targ_ref,
+    halo_hbm,
+    e_send_hbm,
+    e_targ_hbm,
     e_count_ref,
-    p_send_ref,
-    p_targ_ref,
+    p_send_hbm,
+    p_targ_hbm,
     p_count_ref,
-    e_gain_ref,
-    p_gain_ref,
+    e_gain_hbm,
+    p_gain_hbm,
     grid_out,
     mesh_out,
     ext,
@@ -117,11 +121,19 @@
     g_halo,
     peers,
     own,
+    halo_ref,
+    e_send_ref,
+    e_targ_ref,
+    p_send_ref,
+    p_targ_ref,
+    e_gain_ref,
+    p_gain_ref,
     load_sem,
     halo_send,
     halo_recv,
     co_send,
     co_recv,
+    swap_sem,
     rs_send,
     rs_recv,
     back_send,
@@ -132,26 +144,33 @@
     before = lax.rem(patch + n_patch - 1, n_patch)
     grid_rows, mesh_rows = grid_hbm.shape[0], mesh_hbm.shape[0]
     rim = outgoing.shape[0] // 2
-    slots = e_send_ref.shape[1]
+    slots = e_send_ref.shape[0]
     chunk = 256
     mesh_id = pl.DeviceIdType.MESH
 
-    loads = []
     pairs = (
+        (halo_hbm, halo_ref),
         (grid_hbm, ext.at[0:grid_rows]),
+        (e_send_hbm, e_send_ref),
+        (e_targ_hbm, e_targ_ref),
         (w_src_hbm, w_src),
         (mesh_hbm, mesh_v),
         (w_dst_hbm, w_dst),
+        (p_send_hbm, p_send_ref),
+        (p_targ_hbm, p_targ_ref),
+        (e_gain_hbm, e_gain_ref),
+        (p_gain_hbm, p_gain_ref),
         (w_out_hbm, w_out),
         (p_src_hbm, p_src),
         (p_dst_hbm, p_dst),
         (p_out_hbm, p_out),
         (cot_hbm, cot_v),
     )
-    for n, (src, dst) in enumerate(pairs):
-        copy = pltpu.make_async_copy(src, dst, load_sem.at[n])
-        copy.start()
-        loads.append(copy)
+    loads = [
+        pltpu.make_async_copy(src, dst, load_sem.at[n]) for n, (src, dst) in enumerate(pairs)
+    ]
+    for n in range(5):
+        loads[n].start()
 
     barrier = pltpu.get_barrier_semaphore()
     for neighbour in (before, after):
@@ -166,9 +185,12 @@
 
     lax.fori_loop(1, n_group, greet, 0)
 
-    halo_row = halo_ref[...]
+    loads[0].wait()
+    halo_row = halo_ref[...].reshape(1, 2 * rim)
     onehot_cols(hot_h, column(halo_row), 0, grid_rows, 0)
-    loads[0].wait()
+    for n in range(5, len(pairs)):
+        loads[n].start()
+    loads[1].wait()
     outgoing[...] = mm(hot_h[...], ext[0:grid_rows, :]).astype(BF16)
     pl.semaphore_wait(barrier, n_group + 1)
 
@@ -201,17 +223,19 @@
 
     slot = lax.broadcasted_iota(jnp.int32, (1, slots), 1)
     own1 = grid_rows + mesh_rows
-    sender = e_send_ref[...]
+    for n in (2, 3):
+        loads[n].wait()
+    sender = e_send_ref[...].reshape(1, slots)
     sender = jnp.where(sender >= grid_rows, sender + mesh_rows, sender)
-    target = jnp.where(slot < e_count_ref[0], e_targ_ref[...], -1)
+    target = jnp.where(slot < e_count_ref[0], e_targ_ref[...].reshape(1, slots), -1)
     sender_col, target_col = column(sender), column(target)
     onehot_cols(hot1, sender_col, 0, grid_rows, 0)
     onehot_cols(hot1, target_col, grid_rows, own1, grid_rows)
     onehot_cols(hot1, sender_col, own1, own1 + 2 * rim, 0)
-    loads[1].wait()
+    loads[4].wait()
     tbl1[0:grid_rows, :] = mm(ext[0:grid_rows, :], w_src[...]).astype(BF16)
-    loads[2].wait()
-    loads[3].wait()
+    loads[5].wait()
+    loads[6].wait()
     tbl1[grid_rows:own1, :] = mm(mesh_v[...], w_dst[...]).astype(BF16)
 
     def chunks(body):
@@ -228,12 +252,17 @@
     onehot_rows(hot1t, sender, 0, grid_rows, 0)
     onehot_rows(hot1t, target, grid_rows, own1, grid_rows)
     onehot_rows(hot1t, sender, own1, own1 + 2 * rim, 0)
-    p_sender = p_send_ref[...]
-    p_sender = jnp.where(p_sender >= mesh_rows, p_sender + mesh_rows, p_sender)
-    p_target = jnp.where(slot < p_count_ref[0], p_targ_ref[...], -1)
-    p_sender_col, p_target_col = column(p_sender), column(p_target)
+    for n in range(7, 11):
+        loads[n].wait()
+    p_sender = p_send_ref[...].reshape(1, slots)
     local2 = 2 * mesh_rows
     all2 = local2 + coarse.shape[0]
+    half = coarse.shape[0] // 2
+    row_c = p_sender - mesh_rows
+    row_c = ((row_c >> 4) & 1) * half + (row_c >> 5) * COARSE + (row_c & 15)
+    p_sender = jnp.where(p_sender >= mesh_rows, row_c + local2, p_sender)
+    p_target = jnp.where(slot < p_count_ref[0], p_targ_ref[...].reshape(1, slots), -1)
+    p_sender_col, p_target_col = column(p_sender), column(p_target)
     onehot_cols(hot2, p_sender_col, 0, mesh_rows, 0)
     onehot_cols(hot2, p_target_col, mesh_rows, local2, mesh_rows)
     onehot_cols(hot2, p_sender_col, local2, all2, 0)
@@ -250,47 +279,70 @@
 
     def late1(rows):
         preact = acc[rows, :] + mm(hot1[rows, own1 : own1 + 2 * rim], tbl1[own1 : own1 + 2 * rim, :])
-        hidden, slope = silu_pair(preact)
-        hid[rows, :] = hidden.astype(BF16)
-        slope1[rows, :] = slope
+        hid[rows, :] = silu(preact).astype(BF16)
+        slope1[rows, :] = preact
 
     chunks(late1)
-    for n in range(4, len(pairs)):
+    for n in range(11, len(pairs)):
         loads[n].wait()
     summed = mm(hot1t[grid_rows:own1, :], hid[...]).astype(BF16)
     normed1, inverse1 = norm_forward(mm(summed, w_out[...]))
     normed[...] = normed1
     inv[...] = jnp.broadcast_to(inverse1, inv.shape)
-    updated = (mesh_v[...].astype(F32) + normed1 * e_gain_ref[...]).astype(BF16)
+    updated = (mesh_v[...].astype(F32) + normed1 * e_gain_ref[...].reshape(1, -1)).astype(BF16)
     projected = mm(updated, p_src[...]).astype(BF16)
     tbl2[0:mesh_rows, :] = projected
-    own_rows = pl.ds(pl.multiple_of(group * COARSE, COARSE), COARSE)
-
-    def coarse_copy(k):
-        return remote(
+    core, level = lax.rem(group, 2), group // 2
+    partner = group + 1 - 2 * core
+    levels = n_group // 2
+
+    def rows_of(c, z):
+        return pl.ds(pl.multiple_of(c * half + z * COARSE, COARSE), COARSE)
+
+    def level_at(k):
+        return lax.rem(level + k, levels)
+
+    own_rows = rows_of(core, level)
+    far_first = sorted(range(1, levels), key=lambda k: -min(k, levels - k))
+    give = remote(
+        tbl2.at[0:COARSE], coarse.at[own_rows], co_send.at[0], co_recv.at[0], {"group": partner}
+    )
+    spread, relay = {}, {}
+    for k in far_first:
+        spread[k] = remote(
             tbl2.at[0:COARSE],
             coarse.at[own_rows],
-            co_send.at[k - 1],
-            co_recv.at[k - 1],
-            {"group": lax.rem(group + k, n_group)},
+            co_send.at[k],
+            co_recv.at[k],
+            {"group": 2 * level_at(k) + core},
         )
-
-    def each_peer(body):
-        def step(k, carry):
-            body(k)
-            return carry
-
-        lax.fori_loop(1, n_group, step, 0)
-
-    each_peer(lambda k: coarse_copy(k).start())
+        got = rows_of(core, level_at(levels - k))
+        relay[k] = remote(
+            coarse.at[got],
+            coarse.at[got],
+            co_send.at[levels + k],
+            co_recv.at[levels + k],
+            {"group": partner},
+        )
+    for k in far_first:
+        spread[k].start()
+    give.start()
     coarse[own_rows, :] = projected[0:COARSE, :]
     tbl2[mesh_rows:local2, :] = mm(updated, p_dst[...]).astype(BF16)
 
     def early2(rows):
         acc[rows, :] = mm(hot2[rows, 0:local2], tbl2[...])
+        slope1[rows, :] = silu_pair(slope1[rows, :])[1]
 
     chunks(early2)
-    each_peer(lambda k: coarse_copy(k).wait())
+    for k in reversed(far_first):
+        spread[k].wait_recv()
+        relay[k].start()
+    give.wait()
+    for k in far_first:
+        spread[k].wait_send()
+    for k in reversed(far_first):
+        relay[k].wait()
 
     def late2(rows):
         preact = acc[rows, :] + mm(hot2[rows, local2:all2], coarse[...])
@@ -302,7 +354,7 @@
     summed2 = mm(hot2t[mesh_rows:local2, :], hid[...]).astype(BF16)
     normed2, inverse2 = norm_forward(mm(summed2, p_out[...]))
     cot = cot_v[...].astype(F32)
-    node2 = norm_backward(cot * p_gain_ref[...], normed2, inverse2).astype(BF16)
+    node2 = norm_backward(cot * p_gain_ref[...].reshape(1, -1), normed2, inverse2).astype(BF16)
     gnode[...] = mm_t(node2, p_out[...]).astype(BF16)
 
     def back2(rows):
@@ -310,24 +362,32 @@
         gpre[rows, :] = (grad * slope2[rows, :]).astype(BF16)
 
     chunks(back2)
-    gcoarse[...] = mm(hot2t[local2:all2, :], gpre[...]).astype(BF16)
-
-    def rs_copy(k):
-        peer = lax.rem(group + k, n_group)
-        return remote(
-            gcoarse.at[pl.ds(pl.multiple_of(peer * COARSE, COARSE), COARSE)],
+    mine = pl.ds(pl.multiple_of(core * half, COARSE), half)
+    other = pl.ds(pl.multiple_of((1 - core) * half, COARSE), half)
+    swap = remote(gcoarse.at[0], gcoarse.at[1], swap_sem.at[0], swap_sem.at[1], {"group": partner})
+    hot2c = hot2t.at[local2:all2]
+    gcoarse[0] = mm(hot2c[other, :], gpre[...]).astype(BF16)
+    swap.start()
+    part = mm(hot2c[mine, :], gpre[...])
+    g_local = mm(hot2t[0:mesh_rows, :], gpre[...]).astype(BF16)
+    swap.wait()
+    gcoarse[2] = (part + gcoarse[1].astype(F32)).astype(BF16)
+    scatter = {}
+    for k in far_first:
+        to = level_at(k)
+        scatter[k] = remote(
+            gcoarse.at[2, pl.ds(pl.multiple_of(to * COARSE, COARSE), COARSE)],
             rs_buf.at[k - 1],
             rs_send.at[k - 1],
             rs_recv.at[k - 1],
-            {"group": peer},
+            {"group": 2 * to + core},
         )
-
-    each_peer(lambda k: rs_copy(k).start())
-    g_local = mm(hot2t[0:mesh_rows, :], gpre[...]).astype(BF16)
+    for k in far_first:
+        scatter[k].start()
     g_dest = mm(hot2t[mesh_rows:local2, :], gpre[...]).astype(BF16)
     grad_up = cot + mm_t(g_local, p_src[...]) + mm_t(g_dest, p_dst[...])
     gup[...] = grad_up
-    gain = e_gain_ref[...]
+    gain = e_gain_ref[...].reshape(1, -1)
     node1 = norm_backward(grad_up * gain, normed[...], inv[:, 0:1])
     row = lax.broadcasted_iota(jnp.int32, node1.shape, 0)
     node1 = jnp.where(row < COARSE, 0.0, node1).astype(BF16)
@@ -338,10 +398,11 @@
 
     chunks(early3)
     gnode16[...] = jnp.zeros_like(gnode16)
-    each_peer(lambda k: rs_copy(k).wait())
-
-    total = gcoarse[own_rows, :].astype(F32)
-    for k in range(n_group - 1):
+    for k in far_first:
+        scatter[k].wait()
+
+    total = gcoarse[2, pl.ds(pl.multiple_of(level * COARSE, COARSE), COARSE), :].astype(F32)
+    for k in range(levels - 1):
         total = total + rs_buf[k].astype(F32)
     high = total.astype(BF16)
     low = (total - high.astype(F32)).astype(BF16)
@@ -410,9 +471,9 @@
     h2 = halo_rows.shape[0]
     e = encoder_sender.shape[0]
     nc = n_group * COARSE
-    hbm = pl.BlockSpec(memory_space=pl.ANY)
+    hbm = pl.BlockSpec(memory_space=pltpu.MemorySpace.HBM)
+    smem = pl.BlockSpec(memory_space=pltpu.SMEM)
     vmem = pl.BlockSpec(memory_space=pltpu.VMEM)
-    smem = pl.BlockSpec(memory_space=pltpu.SMEM)
     dma = pltpu.SemaphoreType.DMA
     out = pl.pallas_call(
         functools.partial(kernel, n_patch, n_group),
@@ -420,7 +481,7 @@
             jax.ShapeDtypeStruct((g, d), BF16),
             jax.ShapeDtypeStruct((m, d), BF16),
         ),
-        in_specs=[hbm] * 9 + [vmem, vmem, vmem, smem, vmem, vmem, smem, vmem, vmem],
+        in_specs=[hbm] * 12 + [smem] + [hbm] * 2 + [smem] + [hbm] * 2,
         out_specs=(vmem, vmem),
         scratch_shapes=[
             pltpu.VMEM((g + h2, d), BF16),
@@ -449,18 +510,26 @@
             pltpu.VMEM((m, d), F32),
             pltpu.VMEM((m, d), BF16),
             pltpu.VMEM((LANES, d), BF16),
-            pltpu.VMEM((nc, d), BF16),
-            pltpu.VMEM((n_group - 1, COARSE, d), BF16),
+            pltpu.VMEM((3, nc // 2, d), BF16),
+            pltpu.VMEM((n_group // 2 - 1, COARSE, d), BF16),
             pltpu.VMEM((h2, d), BF16),
             pltpu.VMEM((h2, d), BF16),
             pltpu.VMEM((g, d), F32),
-            dma((9,)),
+            pltpu.VMEM((h2,), jnp.int32),
+            pltpu.VMEM((e,), jnp.int32),
+            pltpu.VMEM((e,), jnp.int32),
+            pltpu.VMEM((e,), jnp.int32),
+            pltpu.VMEM((e,), jnp.int32),
+            pltpu.VMEM((d,), F32),
+            pltpu.VMEM((d,), F32),
+            dma((16,)),
             dma((2,)),
             dma((2,)),
-            dma((n_group - 1,)),
-            dma((n_group - 1,)),
-            dma((n_group - 1,)),
-            dma((n_group - 1,)),
+            dma((n_group,)),
+            dma((n_group,)),
+            dma((2,)),
+            dma((n_group // 2 - 1,)),
+            dma((n_group // 2 - 1,)),
             dma((2,)),
             dma((2,)),
         ],
@@ -469,6 +538,9 @@
         ),
         name="step",
     )(
+        *[
+            x if x.size == 1 else pltpu.with_memory_space_constraint(x, pltpu.MemorySpace.HBM)
+            for x in (
         grid_latent,
         mesh_latent,
         cotangent,
@@ -478,15 +550,17 @@
         process_source,
         process_dest,
         process_output,
-        halo_rows.reshape(1, h2),
-        encoder_sender.reshape(1, e),
-        encoder_target.reshape(1, e),
+        halo_rows,
+        encoder_sender,
+        encoder_target,
         encoder_count,
-        process_sender.reshape(1, e),
-        process_target.reshape(1, e),
+        process_sender,
+        process_target,
         process_count,
-        encoder_gain.reshape(1, d),
-        process_gain.reshape(1, d),
+        encoder_gain,
+        process_gain,
+            )
+        ]
     )
     return out
 

time: 66.9 us -> 49.1 us (0.73)
  local copies, waits for them, and re-layouts: 13.4 us -> 1.5 us
  Pallas kernels: 50.8 us -> 45.5 us
    unnamed x34 -> x2, local copies, waits for them, and re-layouts: 13.4 us -> 1.5 us
    pallas_call x1, Pallas kernels: 50.8 us -> 45.5 us  [on_device(): pl.pallas_call(functools.partial(kernel, n_patch, n_group), out_shape=(ja...]
where the time goes in v2:
time: 49.1 us; the launch traced here: 48.9 us
  Pallas kernels  45.5 us (93%)
  between operations  1.94 us (4%)
  local copies, waits for them, and re-layouts  1.5 us (3%)
    pallas_call x1, Pallas kernels, on_device(): pl.pallas_call(functools.partial(kernel, n_patch, n_group), out_shape=(ja...  45.5 us
    unnamed x2, local copies, waits for them, and re-layouts  1.5 us

profile of v2, /device:TPU:1, one launch (start us, length us, event | category | flops | bytes accessed | tf_op | source)
XLA Modules:
  0.0 48.9 jit_solution(12616036436276283293)
XLA Ops:
  1.9 45.5 %step.1 = (bf16[512,512]{1,0:T(8,128)(2,1)S(1)}, bf16[256,512]{1,0:T(8,128)(2,1)S(1)}) custom-call(bf16[512,512]{1,0:T(8,128)(2,1)} %grid_hbm.1, bf16[256,512]{1,0:T(8,128)(2,1)} %mesh_hbm.1, bf16[256,512]{1,0:T(8,128)(2,1)} %cot_hbm.1, bf16[512,512]{1,0:T(8,128)(2,1)} %w_src_hbm.1, bf16[512,512]{1,0:T(8,128)(2,1)} %w_dst_hbm.1, bf16[512,512]{1,0:T(8,128)(2,1)} %w_out_hbm.1, ...), custom_call_target="tpu_custom_call" | custom-call | tf_op jit(solution)/shard_map/step/pallas_call | solution.py:478
  47.4 0.8 %copy.24 = bf16[512,512]{1,0:T(8,128)(2,1)} copy(bf16[512,512]{1,0:T(8,128)(2,1)S(1)} %get-tuple-element.4) | data formatting | bytes 1048576
  48.2 0.7 %copy.25 = bf16[256,512]{1,0:T(8,128)(2,1)} copy(bf16[256,512]{1,0:T(8,128)(2,1)S(1)} %get-tuple-element.5) | data formatting | bytes 524288

commit v3 on v2

--- a/solution.py
+++ b/solution.py
@@ -76,7 +76,7 @@
     p_src_hbm,
     p_dst_hbm,
     p_out_hbm,
-    halo_hbm,
+    halo_ref,
     e_send_hbm,
     e_targ_hbm,
     e_count_ref,
@@ -87,6 +87,7 @@
     p_gain_hbm,
     grid_out,
     mesh_out,
+    grid_v,
     ext,
     mesh_v,
     cot_v,
@@ -106,6 +107,7 @@
     tbl1,
     tbl2,
     coarse,
+    coarse16,
     acc,
     slope1,
     slope2,
@@ -117,17 +119,18 @@
     gnode,
     gnode16,
     gcoarse,
+    joint,
     rs_buf,
     g_halo,
     peers,
     own,
-    halo_ref,
     e_send_ref,
     e_targ_ref,
     p_send_ref,
     p_targ_ref,
     e_gain_ref,
     p_gain_ref,
+    grid_sem,
     load_sem,
     halo_send,
     halo_recv,
@@ -142,15 +145,13 @@
     patch, group = lax.axis_index("patch"), lax.axis_index("group")
     after = lax.rem(patch + 1, n_patch)
     before = lax.rem(patch + n_patch - 1, n_patch)
-    grid_rows, mesh_rows = grid_hbm.shape[0], mesh_hbm.shape[0]
+    grid_rows, mesh_rows = grid_v.shape[0], mesh_hbm.shape[0]
     rim = outgoing.shape[0] // 2
     slots = e_send_ref.shape[0]
     chunk = 256
     mesh_id = pl.DeviceIdType.MESH
 
     pairs = (
-        (halo_hbm, halo_ref),
-        (grid_hbm, ext.at[0:grid_rows]),
         (e_send_hbm, e_send_ref),
         (e_targ_hbm, e_targ_ref),
         (w_src_hbm, w_src),
@@ -169,30 +170,40 @@
     loads = [
         pltpu.make_async_copy(src, dst, load_sem.at[n]) for n, (src, dst) in enumerate(pairs)
     ]
-    for n in range(5):
-        loads[n].start()
-
+    quarter = grid_rows // 4
+    first = [
+        pltpu.make_async_copy(
+            grid_hbm.at[n * quarter : (n + 1) * quarter],
+            grid_v.at[n * quarter : (n + 1) * quarter],
+            grid_sem.at[n],
+        )
+        for n in range(4)
+    ]
+    for copy in first:
+        copy.start()
     barrier = pltpu.get_barrier_semaphore()
     for neighbour in (before, after):
         pl.semaphore_signal(
             barrier, inc=1, device_id={"patch": neighbour}, device_id_type=mesh_id
         )
 
-    def greet(k, carry):
-        peer = lax.rem(group + k, n_group)
+    core, level = lax.rem(group, 2), group // 2
+    levels = n_group // 2
+    partner = group + 1 - 2 * core
+
+    def level_at(k):
+        return lax.rem(level + k, levels)
+
+    contacts = [partner] + [2 * level_at(k) + core for k in range(1, levels)]
+    for peer in contacts:
         pl.semaphore_signal(barrier, inc=1, device_id={"group": peer}, device_id_type=mesh_id)
-        return carry
-
-    lax.fori_loop(1, n_group, greet, 0)
-
-    loads[0].wait()
+
     halo_row = halo_ref[...].reshape(1, 2 * rim)
     onehot_cols(hot_h, column(halo_row), 0, grid_rows, 0)
-    for n in range(5, len(pairs)):
-        loads[n].start()
-    loads[1].wait()
-    outgoing[...] = mm(hot_h[...], ext[0:grid_rows, :]).astype(BF16)
-    pl.semaphore_wait(barrier, n_group + 1)
+    for copy in first:
+        copy.wait()
+    outgoing[...] = mm(hot_h[...], grid_v[...]).astype(BF16)
+    pl.semaphore_wait(barrier, 2 + len(contacts))
 
     def remote(src, dst, send, recv, where):
         return pltpu.make_async_remote_copy(
@@ -206,24 +217,26 @@
 
     up = remote(
         outgoing.at[rim : 2 * rim],
-        ext.at[grid_rows : grid_rows + rim],
+        ext.at[0:rim],
         halo_send.at[0],
         halo_recv.at[0],
         {"patch": after},
     )
     down = remote(
         outgoing.at[0:rim],
-        ext.at[grid_rows + rim : grid_rows + 2 * rim],
+        ext.at[rim : 2 * rim],
         halo_send.at[1],
         halo_recv.at[1],
         {"patch": before},
     )
     up.start()
     down.start()
+    for copy in loads:
+        copy.start()
 
     slot = lax.broadcasted_iota(jnp.int32, (1, slots), 1)
     own1 = grid_rows + mesh_rows
-    for n in (2, 3):
+    for n in (0, 1):
         loads[n].wait()
     sender = e_send_ref[...].reshape(1, slots)
     sender = jnp.where(sender >= grid_rows, sender + mesh_rows, sender)
@@ -232,18 +245,15 @@
     onehot_cols(hot1, sender_col, 0, grid_rows, 0)
     onehot_cols(hot1, target_col, grid_rows, own1, grid_rows)
     onehot_cols(hot1, sender_col, own1, own1 + 2 * rim, 0)
+    loads[2].wait()
+    tbl1[0:grid_rows, :] = mm(grid_v[...], w_src[...]).astype(BF16)
+    loads[3].wait()
     loads[4].wait()
-    tbl1[0:grid_rows, :] = mm(ext[0:grid_rows, :], w_src[...]).astype(BF16)
-    loads[5].wait()
-    loads[6].wait()
     tbl1[grid_rows:own1, :] = mm(mesh_v[...], w_dst[...]).astype(BF16)
 
     def chunks(body):
-        def step(i, carry):
-            body(pl.ds(pl.multiple_of(i * chunk, chunk), chunk))
-            return carry
-
-        lax.fori_loop(0, slots // chunk, step, 0)
+        for i in range(0, slots, chunk):
+            body(slice(i, i + chunk))
 
     def early1(rows):
         acc[rows, :] = mm(hot1[rows, 0:own1], tbl1[0:own1, :])
@@ -252,7 +262,7 @@
     onehot_rows(hot1t, sender, 0, grid_rows, 0)
     onehot_rows(hot1t, target, grid_rows, own1, grid_rows)
     onehot_rows(hot1t, sender, own1, own1 + 2 * rim, 0)
-    for n in range(7, 11):
+    for n in range(5, 9):
         loads[n].wait()
     p_sender = p_send_ref[...].reshape(1, slots)
     local2 = 2 * mesh_rows
@@ -273,9 +283,7 @@
 
     up.wait()
     down.wait()
-    tbl1[own1 : own1 + 2 * rim, :] = mm(ext[grid_rows : grid_rows + 2 * rim, :], w_src[...]).astype(
-        BF16
-    )
+    tbl1[own1 : own1 + 2 * rim, :] = mm(ext[...], w_src[...]).astype(BF16)
 
     def late1(rows):
         preact = acc[rows, :] + mm(hot1[rows, own1 : own1 + 2 * rim], tbl1[own1 : own1 + 2 * rim, :])
@@ -283,34 +291,26 @@
         slope1[rows, :] = preact
 
     chunks(late1)
-    for n in range(11, len(pairs)):
+    for n in range(9, len(pairs)):
         loads[n].wait()
-    summed = mm(hot1t[grid_rows:own1, :], hid[...]).astype(BF16)
-    normed1, inverse1 = norm_forward(mm(summed, w_out[...]))
-    normed[...] = normed1
-    inv[...] = jnp.broadcast_to(inverse1, inv.shape)
-    updated = (mesh_v[...].astype(F32) + normed1 * e_gain_ref[...].reshape(1, -1)).astype(BF16)
-    projected = mm(updated, p_src[...]).astype(BF16)
-    tbl2[0:mesh_rows, :] = projected
-    core, level = lax.rem(group, 2), group // 2
-    partner = group + 1 - 2 * core
-    levels = n_group // 2
+    summed16 = mm(hot1t[grid_rows : grid_rows + COARSE, :], hid[...]).astype(BF16)
+    normed16 = norm_forward(mm(summed16, w_out[...]))[0]
+    mesh16 = mesh_v[0:COARSE, :].astype(F32)
+    updated16 = (mesh16 + normed16 * e_gain_ref[...].reshape(1, -1)).astype(BF16)
+    coarse16[...] = mm(updated16, p_src[...]).astype(BF16)
 
     def rows_of(c, z):
         return pl.ds(pl.multiple_of(c * half + z * COARSE, COARSE), COARSE)
-
-    def level_at(k):
-        return lax.rem(level + k, levels)
 
     own_rows = rows_of(core, level)
     far_first = sorted(range(1, levels), key=lambda k: -min(k, levels - k))
     give = remote(
-        tbl2.at[0:COARSE], coarse.at[own_rows], co_send.at[0], co_recv.at[0], {"group": partner}
+        coarse16, coarse.at[own_rows], co_send.at[0], co_recv.at[0], {"group": partner}
     )
     spread, relay = {}, {}
     for k in far_first:
         spread[k] = remote(
-            tbl2.at[0:COARSE],
+            coarse16,
             coarse.at[own_rows],
             co_send.at[k],
             co_recv.at[k],
@@ -327,7 +327,14 @@
     for k in far_first:
         spread[k].start()
     give.start()
-    coarse[own_rows, :] = projected[0:COARSE, :]
+    coarse[own_rows, :] = coarse16[...]
+    summed = mm(hot1t[grid_rows:own1, :], hid[...]).astype(BF16)
+    normed1, inverse1 = norm_forward(mm(summed, w_out[...]))
+    normed[...] = normed1
+    inv[...] = jnp.broadcast_to(inverse1, inv.shape)
+    updated = (mesh_v[...].astype(F32) + normed1 * e_gain_ref[...].reshape(1, -1)).astype(BF16)
+    projected = mm(updated, p_src[...]).astype(BF16)
+    tbl2[0:mesh_rows, :] = projected
     tbl2[mesh_rows:local2, :] = mm(updated, p_dst[...]).astype(BF16)
 
     def early2(rows):
@@ -368,22 +375,23 @@
     hot2c = hot2t.at[local2:all2]
     gcoarse[0] = mm(hot2c[other, :], gpre[...]).astype(BF16)
     swap.start()
-    part = mm(hot2c[mine, :], gpre[...])
+    gcoarse[2] = mm(hot2c[mine, :], gpre[...]).astype(BF16)
     g_local = mm(hot2t[0:mesh_rows, :], gpre[...]).astype(BF16)
     swap.wait()
-    gcoarse[2] = (part + gcoarse[1].astype(F32)).astype(BF16)
     scatter = {}
-    for k in far_first:
+    for k in far_first + [0]:
         to = level_at(k)
-        scatter[k] = remote(
-            gcoarse.at[2, pl.ds(pl.multiple_of(to * COARSE, COARSE), COARSE)],
-            rs_buf.at[k - 1],
-            rs_send.at[k - 1],
-            rs_recv.at[k - 1],
-            {"group": 2 * to + core},
-        )
-    for k in far_first:
-        scatter[k].start()
+        rows = pl.ds(pl.multiple_of(to * COARSE, COARSE), COARSE)
+        joint[k] = (gcoarse[2, rows, :].astype(F32) + gcoarse[1, rows, :].astype(F32)).astype(BF16)
+        if k:
+            scatter[k] = remote(
+                joint.at[k],
+                rs_buf.at[k - 1],
+                rs_send.at[k - 1],
+                rs_recv.at[k - 1],
+                {"group": 2 * to + core},
+            )
+            scatter[k].start()
     g_dest = mm(hot2t[mesh_rows:local2, :], gpre[...]).astype(BF16)
     grad_up = cot + mm_t(g_local, p_src[...]) + mm_t(g_dest, p_dst[...])
     gup[...] = grad_up
@@ -401,7 +409,7 @@
     for k in far_first:
         scatter[k].wait()
 
-    total = gcoarse[2, pl.ds(pl.multiple_of(level * COARSE, COARSE), COARSE), :].astype(F32)
+    total = joint[0].astype(F32)
     for k in range(levels - 1):
         total = total + rs_buf[k].astype(F32)
     high = total.astype(BF16)
@@ -438,10 +446,23 @@
     own[...] = mm_t(g_own, w_src[...])
     g_targ = mm(hot1t[grid_rows:own1, :], gpre[...]).astype(BF16)
     mesh_out[...] = (gup[...] + mm_t(g_targ, w_dst[...])).astype(BF16)
+    back_down.wait()
+    returned = mm_t(peers[rim : 2 * rim, :], w_src[...]).astype(BF16)
+    own[...] += mm(hot_ht[:, rim : 2 * rim], returned)
     back_up.wait()
-    back_down.wait()
-    returned = mm_t(peers[...], w_src[...]).astype(BF16)
-    grid_out[...] = (own[...] + mm(hot_ht[...], returned)).astype(BF16)
+    returned = mm_t(peers[0:rim, :], w_src[...]).astype(BF16)
+    grid_out[...] = (own[...] + mm(hot_ht[:, 0:rim], returned)).astype(BF16)
+
+
+def write_out(grid_ref, mesh_ref, grid_out, mesh_out, sem):
+    copies = [
+        pltpu.make_async_copy(grid_ref, grid_out, sem.at[0]),
+        pltpu.make_async_copy(mesh_ref, mesh_out, sem.at[1]),
+    ]
+    for copy in copies:
+        copy.start()
+    for copy in copies:
+        copy.wait()
 
 
 def on_device(
@@ -481,10 +502,11 @@
             jax.ShapeDtypeStruct((g, d), BF16),
             jax.ShapeDtypeStruct((m, d), BF16),
         ),
-        in_specs=[hbm] * 12 + [smem] + [hbm] * 2 + [smem] + [hbm] * 2,
+        in_specs=[hbm] * 9 + [vmem] + [hbm] * 2 + [smem] + [hbm] * 2 + [smem] + [hbm] * 2,
         out_specs=(vmem, vmem),
         scratch_shapes=[
-            pltpu.VMEM((g + h2, d), BF16),
+            pltpu.VMEM((g, d), BF16),
+            pltpu.VMEM((h2, d), BF16),
             pltpu.VMEM((m, d), BF16),
             pltpu.VMEM((m, d), BF16),
         ]
@@ -500,6 +522,7 @@
             pltpu.VMEM((g + m + h2, d), BF16),
             pltpu.VMEM((2 * m, d), BF16),
             pltpu.VMEM((nc, d), BF16),
+            pltpu.VMEM((COARSE, d), BF16),
             pltpu.VMEM((e, d), F32),
             pltpu.VMEM((e, d), F32),
             pltpu.VMEM((e, d), F32),
@@ -511,18 +534,19 @@
             pltpu.VMEM((m, d), BF16),
             pltpu.VMEM((LANES, d), BF16),
             pltpu.VMEM((3, nc // 2, d), BF16),
+            pltpu.VMEM((n_group // 2, COARSE, d), BF16),
             pltpu.VMEM((n_group // 2 - 1, COARSE, d), BF16),
             pltpu.VMEM((h2, d), BF16),
             pltpu.VMEM((h2, d), BF16),
             pltpu.VMEM((g, d), F32),
-            pltpu.VMEM((h2,), jnp.int32),
             pltpu.VMEM((e,), jnp.int32),
             pltpu.VMEM((e,), jnp.int32),
             pltpu.VMEM((e,), jnp.int32),
             pltpu.VMEM((e,), jnp.int32),
             pltpu.VMEM((d,), F32),
             pltpu.VMEM((d,), F32),
-            dma((16,)),
+            dma((4,)),
+            dma((14,)),
             dma((2,)),
             dma((2,)),
             dma((n_group,)),
@@ -539,8 +563,8 @@
         name="step",
     )(
         *[
-            x if x.size == 1 else pltpu.with_memory_space_constraint(x, pltpu.MemorySpace.HBM)
-            for x in (
+            x if n in (9, 12, 15) else pltpu.with_memory_space_constraint(x, pltpu.MemorySpace.HBM)
+            for n, x in enumerate((
         grid_latent,
         mesh_latent,
         cotangent,
@@ -559,10 +583,18 @@
         process_count,
         encoder_gain,
         process_gain,
-            )
+            ))
         ]
     )
-    return out
+    out = [pltpu.with_memory_space_constraint(x, pltpu.MemorySpace.VMEM) for x in out]
+    return pl.pallas_call(
+        write_out,
+        out_shape=(jax.ShapeDtypeStruct((g, d), BF16), jax.ShapeDtypeStruct((m, d), BF16)),
+        in_specs=[vmem, vmem],
+        out_specs=(hbm, hbm),
+        scratch_shapes=[dma((2,))],
+        name="write_out",
+    )(*out)
 
 
 def solution(mesh):

time: 49.1 us -> 45.1 us (0.919)
  Pallas kernels: 45.5 us -> 43 us
  local copies, waits for them, and re-layouts: 1.5 us -> 0.01 us
    pallas_call x1, Pallas kernels: 45.5 us -> 42.1 us  [on_device(): pl.pallas_call(functools.partial(kernel, n_patch, n_group), out_shape=(ja...]
    unnamed x2, local copies, waits for them, and re-layouts: 1.5 us -> 0.01 us
    pallas_call x0 -> x1, Pallas kernels: none -> 0.89 us  [on_device(): pl.pallas_call(write_out, out_shape=(jax.ShapeDtypeStruct((g, d), BF16),...]
where the time goes in v3:
time: 45.1 us; the launch traced here: 44.9 us
  Pallas kernels  43 us (95%)
  between operations  1.96 us (4%)
    pallas_call x1, Pallas kernels, on_device(): pl.pallas_call(functools.partial(kernel, n_patch, n_group), out_shape=(ja...  42.1 us

profile of v3, /device:TPU:1, one launch (start us, length us, event | category | flops | bytes accessed | tf_op | source)
XLA Modules:
  0.0 44.9 jit_solution(8425510066694690093)
XLA Ops:
  1.3 0.0 copy-start
  2.0 0.0 copy-done
  2.0 42.1 %step.1 = (bf16[512,512]{1,0:T(8,128)(2,1)S(1)}, bf16[256,512]{1,0:T(8,128)(2,1)S(1)}) custom-call(bf16[512,512]{1,0:T(8,128)(2,1)} %grid_hbm.1, bf16[256,512]{1,0:T(8,128)(2,1)} %mesh_hbm.1, bf16[256,512]{1,0:T(8,128)(2,1)} %cot_hbm.1, bf16[512,512]{1,0:T(8,128)(2,1)} %w_src_hbm.1, bf16[512,512]{1,0:T(8,128)(2,1)} %w_dst_hbm.1, bf16[512,512]{1,0:T(8,128)(2,1)} %w_out_hbm.1, ...), custom_call_target="tpu_custom_call" | custom-call | tf_op jit(solution)/shard_map/step/pallas_call | solution.py:499
  44.0 0.9 %write_out.1 = (bf16[512,512]{1,0:T(8,128)(2,1)}, bf16[256,512]{1,0:T(8,128)(2,1)}) custom-call(bf16[512,512]{1,0:T(8,128)(2,1)S(1)} %get-tuple-element.4.grid_ref, bf16[256,512]{1,0:T(8,128)(2,1)S(1)} %get-tuple-element.5.mesh_ref), custom_call_target="tpu_custom_call" | custom-call | tf_op jit(solution)/shard_map/write_out/pallas_call | solution.py:590
Async XLA Ops:
  1.3 0.7 %copy-start = (s32[256]{0:T(256)S(1)}, s32[256]{0:T(256)}, u32[]{:S(2)}) copy-start(s32[256]{0:T(256)} %halo_ref.1) | copy-start | bytes 3076

commit v4 on v3

--- a/solution.py
+++ b/solution.py
@@ -148,8 +148,22 @@
     grid_rows, mesh_rows = grid_v.shape[0], mesh_hbm.shape[0]
     rim = outgoing.shape[0] // 2
     slots = e_send_ref.shape[0]
-    chunk = 256
+    chunk = 384
     mesh_id = pl.DeviceIdType.MESH
+
+    core, level = lax.rem(group, 2), group // 2
+    levels = n_group // 2
+    partner = group + 1 - 2 * core
+
+    def level_at(k):
+        return lax.rem(level + k, levels)
+
+    far_first = sorted(range(1, levels), key=lambda k: -min(k, levels - k))
+    contacts = [{"group": 2 * level_at(k) + core} for k in far_first]
+    contacts += [{"patch": before}, {"patch": after}, {"group": partner}]
+    barrier = pltpu.get_barrier_semaphore()
+    for where in contacts:
+        pl.semaphore_signal(barrier, inc=1, device_id=where, device_id_type=mesh_id)
 
     pairs = (
         (e_send_hbm, e_send_ref),
@@ -179,31 +193,16 @@
         )
         for n in range(4)
     ]
-    for copy in first:
+    for copy in first + [loads[2]]:
         copy.start()
-    barrier = pltpu.get_barrier_semaphore()
-    for neighbour in (before, after):
-        pl.semaphore_signal(
-            barrier, inc=1, device_id={"patch": neighbour}, device_id_type=mesh_id
-        )
-
-    core, level = lax.rem(group, 2), group // 2
-    levels = n_group // 2
-    partner = group + 1 - 2 * core
-
-    def level_at(k):
-        return lax.rem(level + k, levels)
-
-    contacts = [partner] + [2 * level_at(k) + core for k in range(1, levels)]
-    for peer in contacts:
-        pl.semaphore_signal(barrier, inc=1, device_id={"group": peer}, device_id_type=mesh_id)
 
     halo_row = halo_ref[...].reshape(1, 2 * rim)
     onehot_cols(hot_h, column(halo_row), 0, grid_rows, 0)
-    for copy in first:
+    for copy in first + [loads[2]]:
         copy.wait()
-    outgoing[...] = mm(hot_h[...], grid_v[...]).astype(BF16)
-    pl.semaphore_wait(barrier, 2 + len(contacts))
+    tbl1[0:grid_rows, :] = mm(grid_v[...], w_src[...]).astype(BF16)
+    outgoing[...] = mm(hot_h[...], tbl1[0:grid_rows, :]).astype(BF16)
+    pl.semaphore_wait(barrier, len(contacts))
 
     def remote(src, dst, send, recv, where):
         return pltpu.make_async_remote_copy(
@@ -231,7 +230,7 @@
     )
     up.start()
     down.start()
-    for copy in loads:
+    for copy in loads[:2] + loads[3:]:
         copy.start()
 
     slot = lax.broadcasted_iota(jnp.int32, (1, slots), 1)
@@ -245,8 +244,6 @@
     onehot_cols(hot1, sender_col, 0, grid_rows, 0)
     onehot_cols(hot1, target_col, grid_rows, own1, grid_rows)
     onehot_cols(hot1, sender_col, own1, own1 + 2 * rim, 0)
-    loads[2].wait()
-    tbl1[0:grid_rows, :] = mm(grid_v[...], w_src[...]).astype(BF16)
     loads[3].wait()
     loads[4].wait()
     tbl1[grid_rows:own1, :] = mm(mesh_v[...], w_dst[...]).astype(BF16)
@@ -283,10 +280,8 @@
 
     up.wait()
     down.wait()
-    tbl1[own1 : own1 + 2 * rim, :] = mm(ext[...], w_src[...]).astype(BF16)
-
     def late1(rows):
-        preact = acc[rows, :] + mm(hot1[rows, own1 : own1 + 2 * rim], tbl1[own1 : own1 + 2 * rim, :])
+        preact = acc[rows, :] + mm(hot1[rows, own1 : own1 + 2 * rim], ext[...])
         hid[rows, :] = silu(preact).astype(BF16)
         slope1[rows, :] = preact
 
@@ -303,7 +298,6 @@
         return pl.ds(pl.multiple_of(c * half + z * COARSE, COARSE), COARSE)
 
     own_rows = rows_of(core, level)
-    far_first = sorted(range(1, levels), key=lambda k: -min(k, levels - k))
     give = remote(
         coarse16, coarse.at[own_rows], co_send.at[0], co_recv.at[0], {"group": partner}
     )
@@ -519,7 +513,7 @@
             pltpu.VMEM((g + m + h2, e), BF16),
             pltpu.VMEM((e, 2 * m + nc), BF16),
             pltpu.VMEM((2 * m + nc, e), BF16),
-            pltpu.VMEM((g + m + h2, d), BF16),
+            pltpu.VMEM((g + m, d), BF16),
             pltpu.VMEM((2 * m, d), BF16),
             pltpu.VMEM((nc, d), BF16),
             pltpu.VMEM((COARSE, d), BF16),

time: 45.1 us -> 45.2 us (level)
  no operation moved by 1% of the time
where the time goes in v4:
time: 45.2 us; the launch traced here: 45 us
  Pallas kernels  43 us (95%)
  between operations  1.96 us (4%)
    pallas_call x1, Pallas kernels, on_device(): pl.pallas_call(functools.partial(kernel, n_patch, n_group), out_shape=(ja...  42.1 us

profile of v4, /device:TPU:1, one launch (start us, length us, event | category | flops | bytes accessed | tf_op | source)
XLA Modules:
  0.0 45.0 jit_solution(7836009450474069681)
XLA Ops:
  1.3 0.0 copy-start
  2.0 0.0 copy-done
  2.0 42.1 %step.1 = (bf16[512,512]{1,0:T(8,128)(2,1)S(1)}, bf16[256,512]{1,0:T(8,128)(2,1)S(1)}) custom-call(bf16[512,512]{1,0:T(8,128)(2,1)} %grid_hbm.1, bf16[256,512]{1,0:T(8,128)(2,1)} %mesh_hbm.1, bf16[256,512]{1,0:T(8,128)(2,1)} %cot_hbm.1, bf16[512,512]{1,0:T(8,128)(2,1)} %w_src_hbm.1, bf16[512,512]{1,0:T(8,128)(2,1)} %w_dst_hbm.1, bf16[512,512]{1,0:T(8,128)(2,1)} %w_out_hbm.1, ...), custom_call_target="tpu_custom_call" | custom-call | tf_op jit(solution)/shard_map/step/pallas_call | solution.py:493
  44.1 0.9 %write_out.1 = (bf16[512,512]{1,0:T(8,128)(2,1)}, bf16[256,512]{1,0:T(8,128)(2,1)}) custom-call(bf16[512,512]{1,0:T(8,128)(2,1)S(1)} %get-tuple-element.4.grid_ref, bf16[256,512]{1,0:T(8,128)(2,1)S(1)} %get-tuple-element.5.mesh_ref), custom_call_target="tpu_custom_call" | custom-call | tf_op jit(solution)/shard_map/write_out/pallas_call | solution.py:584
Async XLA Ops:
  1.3 0.7 %copy-start = (s32[256]{0:T(256)S(1)}, s32[256]{0:T(256)}, u32[]{:S(2)}) copy-start(s32[256]{0:T(256)} %halo_ref.1) | copy-start | bytes 3076

commit v5 on v4

--- a/solution.py
+++ b/solution.py
@@ -148,7 +148,7 @@
     grid_rows, mesh_rows = grid_v.shape[0], mesh_hbm.shape[0]
     rim = outgoing.shape[0] // 2
     slots = e_send_ref.shape[0]
-    chunk = 384
+    chunk = 256
     mesh_id = pl.DeviceIdType.MESH
 
     core, level = lax.rem(group, 2), group // 2
@@ -449,10 +449,12 @@
 
 
 def write_out(grid_ref, mesh_ref, grid_out, mesh_out, sem):
-    copies = [
-        pltpu.make_async_copy(grid_ref, grid_out, sem.at[0]),
-        pltpu.make_async_copy(mesh_ref, mesh_out, sem.at[1]),
-    ]
+    piece = 128
+    copies = []
+    for src, dst in ((grid_ref, grid_out), (mesh_ref, mesh_out)):
+        for lo in range(0, src.shape[0], piece):
+            rows = slice(lo, lo + piece)
+            copies.append(pltpu.make_async_copy(src.at[rows], dst.at[rows], sem.at[len(copies)]))
     for copy in copies:
         copy.start()
     for copy in copies:
@@ -586,7 +588,7 @@
         out_shape=(jax.ShapeDtypeStruct((g, d), BF16), jax.ShapeDtypeStruct((m, d), BF16)),
         in_specs=[vmem, vmem],
         out_specs=(hbm, hbm),
-        scratch_shapes=[dma((2,))],
+        scratch_shapes=[dma(((g + m) // 128,))],
         name="write_out",
     )(*out)
 

time: 45.2 us -> 45.1 us (level)
  no operation moved by 1% of the time
where the time goes in v5:
time: 45.1 us; the launch traced here: 44.9 us
  Pallas kernels  43 us (95%)
  between operations  1.96 us (4%)
    pallas_call x1, Pallas kernels, on_device(): pl.pallas_call(functools.partial(kernel, n_patch, n_group), out_shape=(ja...  42 us
    pallas_call x1, Pallas kernels, on_device(): pl.pallas_call(write_out, out_shape=(jax.ShapeDtypeStruct((g, d), BF16),...  0.93 us

profile of v5, /device:TPU:1, one launch (start us, length us, event | category | flops | bytes accessed | tf_op | source)
XLA Modules:
  0.0 44.9 jit_solution(4384238600257711084)
XLA Ops:
  1.3 0.0 copy-start
  2.0 0.0 copy-done
  2.0 42.0 %step.1 = (bf16[512,512]{1,0:T(8,128)(2,1)S(1)}, bf16[256,512]{1,0:T(8,128)(2,1)S(1)}) custom-call(bf16[512,512]{1,0:T(8,128)(2,1)} %grid_hbm.1, bf16[256,512]{1,0:T(8,128)(2,1)} %mesh_hbm.1, bf16[256,512]{1,0:T(8,128)(2,1)} %cot_hbm.1, bf16[512,512]{1,0:T(8,128)(2,1)} %w_src_hbm.1, bf16[512,512]{1,0:T(8,128)(2,1)} %w_dst_hbm.1, bf16[512,512]{1,0:T(8,128)(2,1)} %w_out_hbm.1, ...), custom_call_target="tpu_custom_call" | custom-call | tf_op jit(solution)/shard_map/step/pallas_call | solution.py:495
  44.0 0.9 %write_out.1 = (bf16[512,512]{1,0:T(8,128)(2,1)}, bf16[256,512]{1,0:T(8,128)(2,1)}) custom-call(bf16[512,512]{1,0:T(8,128)(2,1)S(1)} %get-tuple-element.4.grid_ref, bf16[256,512]{1,0:T(8,128)(2,1)S(1)} %get-tuple-element.5.mesh_ref), custom_call_target="tpu_custom_call" | custom-call | tf_op jit(solution)/shard_map/write_out/pallas_call | solution.py:586
Async XLA Ops:
  1.3 0.7 %copy-start = (s32[256]{0:T(256)S(1)}, s32[256]{0:T(256)}, u32[]{:S(2)}) copy-start(s32[256]{0:T(256)} %halo_ref.1) | copy-start | bytes 3076
